TPU v7x, 128 devices: a whole 4x4x4 slice. The times are simulated.
128 devices in a mesh: group: 8 (over y, core), member: 16 (over z, x).
Axes of the slice: x: 4, y: 4, z: 4, core: 2. Of those that a mesh axis runs over, the one named last changes fastest.
Arguments:
- hidden: bfloat16 [49152, 3584], P(('group', 'member')), may hold values from -30 to 30
- projection: bfloat16 [3584, 1024], replicated, may hold values from -0.09375 to 0.09375
- inv_temp: float32 [1], replicated, may hold values from 10 to 80
- partners: int32 [128, 12], P(('group', 'member')), may hold values from 0 to 127, as said below
- positives: int32 [49152], P(('group', 'member')), may hold values from 0 to 49151, as said below
Outputs:
- loss: float32 [], replicated
- grad_hidden: bfloat16 [49152, 3584], P(('group', 'member'))
- grad_proj: float32 [3584, 1024], P(('group', 'member'))
Inputs may be any that keep to these rules, and one draw needn't show every extreme that they name: Block ids are numbered in row order. partners[b] are 12 distinct blocks of b's own group of 16 consecutive blocks, none equal to b; within a group they are b's index in the group XORed with 12 distinct nonzero offsets common to that group, so b lists c exactly when c lists b. positives pairs the rows of each block among themselves: positives_i lies in i's block, differs from i, and positives of positives_i is i.
All inputs are finite; a program needn't handle non-finite values.
Results may differ from a plain program's by a relative error of at most 0.006.
Values may be sent and summed in bfloat16 or wider, within the bound.
No kernel may reach another device: no remote copies, remote signals or barrier semaphores. Data moves between devices by JAX's collectives and lax.ppermute only.
A program may use at most 128 MiB of HBM per device.

v0:
```python
import functools

import jax
import jax.numpy as jnp
from jax import lax
from jax.experimental import pallas as pl
from jax.experimental.pallas import tpu as pltpu
from jax.sharding import Mesh, PartitionSpec as P

epsilon = 1e-06
shift = 3.0
AXES = ("y", "core", "z", "x")
NEAR = [(0, 0), (0, 1), (0, 3), (1, 0), (1, 1), (1, 3), (3, 0), (3, 1), (3, 3)]
FAR = [(0, 2), (1, 2), (3, 2), (2, 0), (2, 1), (2, 2), (2, 3)]


def send(array, axis, step):
    return lax.ppermute(array, axis, [(i, (i + step) % 4) for i in range(4)])


def swap(array):
    return lax.ppermute(array, "core", [(0, 1), (1, 0)])


def ring_gather(block, axis):
    half = block.shape[0] // 2
    back = send(block, axis, 1)
    ahead = send(block, axis, -1)
    far_top = send(back[:half], axis, 1)
    far_bottom = send(ahead[half:], axis, -1)
    return (back,), (far_top, far_bottom), (ahead,)


def ring_total(parts, axis):
    total = parts
    for d in (1, 2, 3):
        seen = send(parts, axis, -d)
        total = total + jnp.roll(seen, -d, axis=0)
    return total


def total_over_y(value):
    for bit in (1, 2):
        value = value + lax.ppermute(value, "y", [(i, i ^ bit) for i in range(4)])
    return value


def target_of(pos):
    rows = pos.shape[0]
    return lax.broadcasted_iota(jnp.int32, (rows, rows), 1) == pos


def score_kernel(tiles, names, pieces, final, *refs):
    active, scale, pos = refs[:3]
    count = sum(pieces)
    row_in, col_in = refs[3 : 3 + count], refs[3 + count : 3 + 2 * count]
    outs = refs[3 + 2 * count :]
    powers, row_sums, col_sums = outs[:3]
    row_units, col_units = outs[-2:]
    rows = pos.shape[0]
    row_sums[...] = jnp.zeros_like(row_sums)
    col_sums[...] = jnp.zeros_like(col_sums)
    for sources, target in ((row_in, row_units), (col_in, col_units)):
        at = 0
        for place, many in enumerate(pieces):
            cut = rows // many
            for part in range(many):
                target[place, cut * part : cut * (part + 1)] = sources[at][...]
                at += 1
    factor = scale[0]
    for place, (dx, dz) in enumerate(tiles):
        scores = factor * lax.dot_general(
            row_units[names.index(dx)],
            col_units[names.index(dz)],
            (((1,), (1,)), ((), ())),
            preferred_element_type=jnp.float32,
        )
        power = jnp.exp(scores - shift)
        if (dx, dz) == (0, 0):
            here = lax.broadcasted_iota(jnp.int32, (rows, rows), 0)
            there = lax.broadcasted_iota(jnp.int32, (rows, rows), 1)
            power = jnp.where(here == there, 0.0, power)
            hit = jnp.where(target_of(pos[...]), scores, 0.0)
            outs[3][...] = hit[:, :128] + hit[:, 128:256] + hit[:, 256:]
        else:
            power = power * active[4 * dx + dz]
        powers[place] = power.astype(jnp.bfloat16)
        row_sums[dx] += power[:, :128] + power[:, 128:256] + power[:, 256:]
        col_sums[dz] += jnp.sum(power.reshape(rows // 8, 8, rows), axis=0)
    if final:
        half = row_units.shape[2] // 2
        for place, d in enumerate(names):
            outs[3][rows * d : rows * (d + 1)] = row_units[place, :, half:]
            outs[4][rows * d : rows * (d + 1)] = col_units[place, :, :half]


def score_tiles(tiles, final, active, scale, pos, row_pieces, col_pieces):
    names = sorted({d for tile in tiles for d in tile})
    rows = pos.shape[0]
    width = row_pieces[0][0].shape[1]
    smem = pl.BlockSpec(memory_space=pltpu.SMEM)
    vmem = pl.BlockSpec(memory_space=pltpu.VMEM)
    out_shape = [
        jax.ShapeDtypeStruct((len(tiles), rows, rows), jnp.bfloat16),
        jax.ShapeDtypeStruct((4, rows, 128), jnp.float32),
        jax.ShapeDtypeStruct((4, 8, rows), jnp.float32),
    ]
    if final:
        out_shape += [jax.ShapeDtypeStruct((4 * rows, width // 2), jnp.bfloat16)] * 2
    else:
        out_shape += [jax.ShapeDtypeStruct((rows, 128), jnp.float32)]
    block = pltpu.VMEM((len(names), rows, width), jnp.bfloat16)
    pieces = [len(row_pieces[d]) for d in names]
    return pl.pallas_call(
        functools.partial(score_kernel, tiles, names, pieces, final),
        out_shape=tuple(out_shape),
        in_specs=[smem, smem] + [vmem] * (1 + 2 * sum(pieces)),
        out_specs=(vmem,) * len(out_shape),
        scratch_shapes=[block, block],
        compiler_params=pltpu.CompilerParams(vmem_limit_bytes=48 << 20),
        cost_estimate=pl.CostEstimate(
            flops=len(tiles) * 2 * rows * rows * width,
            transcendentals=len(tiles) * rows * rows,
            bytes_accessed=16 << 20,
        ),
        name="scores",
    )(
        active, scale, pos,
        *[piece for d in names for piece in row_pieces[d]],
        *[piece for d in names for piece in col_pieces[d]],
    )


def weight_tile(source, place, dx, dz, row_inv, col_inv):
    inv = row_inv[dx]
    return source[place].astype(jnp.float32) * (jnp.concatenate([inv, inv, inv], axis=1) + col_inv[dz])


def product(left, right):
    return jnp.dot(left, right, preferred_element_type=jnp.float32)


def product_over_rows(left, right):
    return lax.dot_general(left, right, (((0,), (0,)), ((), ())), preferred_element_type=jnp.float32)


def far_kernel(row_inv, col_inv, far, rows_right, cols_left, far_row, far_col, wide, tall):
    rows = far.shape[1]
    for place, (dx, dz) in enumerate(FAR):
        weight = weight_tile(far, place, dx, dz, row_inv, col_inv).astype(jnp.bfloat16)
        if dx == 2:
            wide[:, rows * dz : rows * (dz + 1)] = weight
        if dz == 2:
            tall[rows * dx : rows * (dx + 1)] = weight
    far_row[...] = product(wide[...], cols_left[...]).astype(far_row.dtype)
    far_col[...] = product_over_rows(tall[...], rows_right[...]).astype(far_col.dtype)


def own_kernel(pos, row_inv, col_inv, near, wide, tall, rows_right, cols_left, by_row, by_col, weights):
    rows = pos.shape[0]
    weights[2 * rows : 3 * rows] = wide[...]
    weights[:, 2 * rows : 3 * rows] = tall[...]
    for place, (dx, dz) in enumerate(NEAR):
        weight = weight_tile(near, place, dx, dz, row_inv, col_inv)
        if (dx, dz) == (0, 0):
            weight = weight - jnp.where(target_of(pos[...]), 2.0, 0.0)
        weights[rows * dx : rows * (dx + 1), rows * dz : rows * (dz + 1)] = weight.astype(jnp.bfloat16)
    by_row[...] = product(weights[:rows], cols_left[...])
    by_col[...] = product_over_rows(weights[:, :rows], rows_right[...])


def near_kernel(weights, rows_right, cols_left, x_top, x_bottom, z_top, z_bottom, *outs):
    rows = weights.shape[0] // 4
    cut = rows // 2
    for place, d in enumerate((1, 3)):
        span = slice(cut) if d == 1 else slice(cut, rows)
        by_row = product(weights[rows * d : rows * (d + 1)], cols_left[...])
        by_col = product_over_rows(weights[:, rows * d : rows * (d + 1)], rows_right[...])
        for out, made, seen in (
            (outs[place], by_row, (x_top, x_bottom)[place]),
            (outs[2 + place], by_col, (z_top, z_bottom)[place]),
        ):
            out[...] = made.astype(out.dtype)
            out[span] = (made[span] + seen[...].astype(jnp.float32)).astype(out.dtype)


def gather_kernel(names, places, hidden_own, hidden_other, *refs):
    own, other = refs[: len(names)], refs[len(names) : 2 * len(names)]
    total = jnp.zeros((hidden_own.shape[2], own[0].shape[1]), jnp.float32)
    for k, d in enumerate(names):
        total += product_over_rows(hidden_own[places[d]], own[k][...])
        total += product_over_rows(hidden_other[places[d]], other[k][...])
    refs[-1][...] = total


def last_kernel(places, hidden_own, hidden_other, own, other, first, spare, out, total):
    total[...] = (
        first[...]
        + product_over_rows(hidden_own[places[2]], own[...])
        + product_over_rows(hidden_other[places[2]], other[...])
    )
    count, padded = out.shape[:2]
    rows = padded - spare.shape[0]
    for k in range(count):
        out[k, :rows] = total[rows * k : rows * (k + 1)].astype(out.dtype)
        out[k, rows:] = spare[...].astype(out.dtype)


def far_chunks(row_inv, col_inv, far, rows_right, cols_left):
    rows, half = far.shape[1], cols_left.shape[1]
    vmem = pl.BlockSpec(memory_space=pltpu.VMEM)
    chunk = jax.ShapeDtypeStruct((rows, half), jnp.bfloat16)
    return pl.pallas_call(
        far_kernel,
        out_shape=(
            chunk,
            chunk,
            jax.ShapeDtypeStruct((rows, 4 * rows), jnp.bfloat16),
            jax.ShapeDtypeStruct((4 * rows, rows), jnp.bfloat16),
        ),
        in_specs=[vmem] * 5,
        out_specs=(vmem,) * 4,
        compiler_params=pltpu.CompilerParams(vmem_limit_bytes=48 << 20),
        cost_estimate=pl.CostEstimate(
            flops=16 * rows * rows * half, transcendentals=0, bytes_accessed=8 << 20
        ),
        name="far_weights",
    )(row_inv, col_inv, far, rows_right, cols_left)


def call(kernel, name, flops, inputs, out_shape, scratch=(), scalars=0):
    vmem = pl.BlockSpec(memory_space=pltpu.VMEM)
    smem = pl.BlockSpec(memory_space=pltpu.SMEM)
    many = isinstance(out_shape, tuple)
    return pl.pallas_call(
        kernel,
        out_shape=out_shape,
        in_specs=[smem] * scalars + [vmem] * (len(inputs) - scalars),
        out_specs=(vmem,) * len(out_shape) if many else vmem,
        scratch_shapes=scratch,
        compiler_params=pltpu.CompilerParams(vmem_limit_bytes=48 << 20),
        cost_estimate=pl.CostEstimate(flops=flops, transcendentals=0, bytes_accessed=12 << 20),
        name=name,
    )(*inputs)


def per_device(hidden, projection, inv_temp, partners, positives):
    rows = hidden.shape[0]
    width = projection.shape[1]
    half = width // 2
    iy, ic = lax.axis_index("y"), lax.axis_index("core")
    iz, ix = lax.axis_index("z"), lax.axis_index("x")
    mine = iz * 4 + ix

    offsets = (partners[0] % 16) ^ mine
    back = jnp.arange(4)
    row_ids = iz * 4 + (ix - back) % 4
    col_ids = ((iz - back) % 4) * 4 + ix
    apart = (row_ids[:, None] ^ col_ids[None, :]).reshape(16)
    active = (jnp.any(apart[:, None] == offsets[None, :], axis=1) | (apart == 0)).astype(jnp.int32)
    pos = (positives % rows)[:, None]

    projected = jnp.dot(hidden, projection, preferred_element_type=jnp.float32)
    lengths = jnp.sqrt(jnp.sum(projected * projected, axis=1, keepdims=True) + epsilon)
    unit_rows = projected / lengths
    unit_low = unit_rows.astype(jnp.bfloat16)

    x_back, x_far, x_ahead = ring_gather(unit_low, "x")
    z_back, z_far, z_ahead = ring_gather(unit_low, "z")

    fourth = hidden.shape[1] // 4
    by_y = jnp.stack([hidden[:, fourth * k : fourth * (k + 1)] for k in range(4)])
    own_hidden = lax.all_to_all(by_y, "y", 0, 0)

    own = (unit_low,)
    near, near_rows, near_cols, hits = score_tiles(
        NEAR, False, active, inv_temp, pos, {0: own, 1: x_back, 3: x_ahead}, {0: own, 1: z_back, 3: z_ahead}
    )
    far, far_rows, far_cols, rows_right, cols_left = score_tiles(
        FAR,
        True,
        active,
        inv_temp,
        pos,
        {0: own, 1: x_back, 2: x_far, 3: x_ahead},
        {0: own, 1: z_back, 2: z_far, 3: z_ahead},
    )

    row_sums = jnp.sum(near_rows + far_rows, axis=2)
    hit_sum = jnp.full((4, 128), jnp.sum(hits)) * (back == 0)[:, None]
    row_totals = ring_total(jnp.concatenate([row_sums, hit_sum], axis=1), "x")
    row_totals, hit_sum = row_totals[:, :rows], row_totals[:, rows]
    col_totals = ring_total(jnp.sum(near_cols + far_cols, axis=1), "z")
    row_inv = jnp.broadcast_to((1.0 / row_totals)[:, :, None], (4, rows, 128))
    col_inv = (1.0 / col_totals)[:, None, :]
    row_inv, col_inv, own_hidden = lax.optimization_barrier((row_inv, col_inv, own_hidden))
    other_hidden = swap(own_hidden)

    far_row, far_col, wide, tall = far_chunks(row_inv, col_inv, far, rows_right, cols_left)
    cut = rows // 2
    seen = (
        send(far_row[:cut], "x", -1),
        send(far_row[cut:], "x", 1),
        send(far_col[:cut], "z", -1),
        send(far_col[cut:], "z", 1),
    )
    unit = 2 * rows * rows * half
    chunk = jax.ShapeDtypeStruct((rows, half), jnp.float32)
    low_chunk = jax.ShapeDtypeStruct((rows, half), jnp.bfloat16)
    square = jax.ShapeDtypeStruct((4 * rows, 4 * rows), jnp.bfloat16)
    by_row, by_col, weights = call(
        own_kernel, "own_weights", 8 * unit,
        (pos, row_inv, col_inv, near, wide, tall, rows_right, cols_left),
        (chunk, chunk, square),
    )
    x_next, x_last, z_next, z_last = call(
        near_kernel, "near_weights", 16 * unit,
        (weights, rows_right, cols_left, *seen),
        (low_chunk,) * 4,
    )
    x_sum = by_row + send(x_next, "x", -1).astype(jnp.float32) + send(x_last, "x", 1).astype(jnp.float32)
    z_sum = by_col + send(z_next, "z", -1).astype(jnp.float32) + send(z_last, "z", 1).astype(jnp.float32)
    halves = [x_sum, z_sum]
    halves, other_hidden = lax.optimization_barrier((halves, other_hidden))
    grad_unit = inv_temp[0] * jnp.concatenate(halves, axis=1)
    along = jnp.sum(unit_rows * grad_unit, axis=1, keepdims=True)
    grad_projected = ((grad_unit - unit_rows * along) / lengths).astype(jnp.bfloat16)
    grad_hidden = lax.dot_general(
        grad_projected, projection, (((1,), (1,)), ((), ())), preferred_element_type=jnp.float32
    ).astype(jnp.bfloat16)

    ring_loss = jnp.sum(shift + jnp.log(row_totals)) - jnp.sum(hit_sum)
    total = total_over_y(jnp.full((8, 128), ring_loss))

    left, right = grad_projected[:, :half], grad_projected[:, half:]
    kept = jnp.where(ic == 0, left, right)
    other = swap(jnp.where(ic == 0, right, left))
    own_back, other_back = send(kept, "y", 1), send(other, "y", 1)
    own_ahead, other_ahead = send(kept, "y", -1), send(other, "y", -1)
    own_far, other_far = send(own_back, "y", 1), send(other_ahead, "y", -1)
    places = (iy - back) % 4
    step = 2 * rows * fourth * half
    first = call(
        functools.partial(gather_kernel, (0, 1, 3)), "near_rows", 6 * step,
        (places, own_hidden, other_hidden, kept, own_back, own_ahead, other, other_back, other_ahead),
        jax.ShapeDtypeStruct((fourth, half), jnp.float32),
        scalars=1,
    )
    first, own_far, other_far, grad_hidden, total = lax.optimization_barrier(
        (first, own_far, other_far, grad_hidden, total)
    )
    high = lax.reduce_precision(total[0, 0], 8, 7)
    middle = lax.reduce_precision(total[0, 0] - high, 8, 7)
    low = total[0, 0] - high - middle
    spare = jnp.stack([high, middle, low, jnp.zeros_like(low)])
    part = call(
        last_kernel, "last_rows", 2 * step,
        (places, own_hidden, other_hidden, own_far, other_far, first, jnp.broadcast_to(spare[:, None], (4, half))),
        jax.ShapeDtypeStruct((32, fourth // 32 + 4, half), jnp.bfloat16),
        scratch=[pltpu.VMEM((fourth, half), jnp.float32)],
        scalars=1,
    )
    arrived = lax.all_to_all(part, ("core", "z", "x"), 0, 0).astype(jnp.float32)
    sums = jnp.sum(arrived.reshape(2, 16, fourth // 32 + 4, half), axis=1)
    grad_proj = jnp.concatenate([sums[0, : fourth // 32], sums[1, : fourth // 32]], axis=1)
    loss = jnp.sum(sums[:, fourth // 32 :, 0]) / (4 * 128 * rows)
    return (loss, grad_hidden, grad_proj)


def solution(mesh):
    split = Mesh(mesh.devices.reshape(4, 2, 4, 4), AXES)
    return jax.shard_map(
        per_device,
        mesh=split,
        in_specs=(P(AXES, None), P(), P(), P(AXES, None), P(AXES)),
        out_specs=(P(), P(AXES, None), P(AXES, None)),
        check_vma=False,
    )
```

profile of v0, /device:TPU:0, one launch (start us, length us, event | category | flops | bytes accessed | tf_op | source)
XLA Modules:
  0.0 181.5 jit_solution(6735332189402206854)
XLA Ops:
  0.6 6.4 %multiply_reduce_fusion.1 = (f32[384]{0:T(512)S(1)}, f32[384,1024]{1,0:T(8,128)S(1)}) fusion(bf16[384,3584]{1,0:T(8,128)(2,1)} %param.5, bf16[3584,1024]{1,0:T(8,128)(2,1)} %param.6), kind=kOutput, calls=%fused_computation.6 | convolution fusion | flops 2819358208 | bytes 11666944 | tf_op jit(solution)/shard_map/dot_general | solution.py:263
  16.7 4.7 %all-to-all-start = ((bf16[4,384,896]{2,1,0:T(8,128)(2,1)}), bf16[4,384,896]{2,1,0:T(8,128)(2,1)}, u32[]{:S(2)}, u32[]{:S(2)}) async-start(bf16[4,384,896]{2,1,0:T(8,128)(2,1)} %pad_maximum_fusion), calls=%async_computation | async-start | bytes 5505024 | tf_op jit(solution)/shard_map/all_to_all | solution.py:273
  21.9 5.9 %collective-permute-done.refs_4_ = bf16[384,1024]{1,0:T(8,128)(2,1)S(1)} collective-permute-done((bf16[384,1024]{1,0:T(8,128)(2,1)S(1)}, bf16[384,1024]{1,0:T(8,128)(2,1)S(1)}, u32[]{:S(2)}, u32[]{:S(2)}) %collective-permute-start) | collective-permute-done | bytes 786464 | tf_op jit(solution)/shard_map/ppermute | solution.py:18
  29.8 2.8 %collective-permute-start.5 = (bf16[192,1024]{1,0:T(8,128)(2,1)}, bf16[192,1024]{1,0:T(8,128)(2,1)}, u32[]{:S(2)}, u32[]{:S(2)}) collective-permute-start(bf16[192,1024]{1,0:T(8,128)(2,1)} %slice.143), channel_id=1, source_target_pairs={{0,3},{1,0},{2,1},{3,2},{4,7},{5,4},{6,5},{7,6},{8,11},{9,8},{10,9... | collective-permute-start | bytes 1179656 | tf_op jit(solution)/shard_map/ppermute | solution.py:18
  37.3 2.1 %collective-permute-start.7 = (bf16[192,1024]{1,0:T(8,128)(2,1)}, bf16[192,1024]{1,0:T(8,128)(2,1)}, u32[]{:S(2)}, u32[]{:S(2)}) collective-permute-start(bf16[192,1024]{1,0:T(8,128)(2,1)} %slice.145), channel_id=1, source_target_pairs={{0,12},{4,0},{8,4},{12,8},{1,13},{5,1},{9,5},{13,9},{2,14},{6,2},{... | collective-permute-start | bytes 1179656 | tf_op jit(solution)/shard_map/ppermute | solution.py:18
  41.3 6.8 %scores.2 = (bf16[9,384,384]{2,1,0:T(8,128)(2,1)}, f32[4,384,128]{2,1,0:T(8,128)S(1)}, f32[4,8,384]{2,1,0:T(8,128)S(1)}, f32[384,128]{1,0:T(8,128)S(1)}) custom-call(s32[16]{0:T(128)S(1)} %or_convert_fusion.refs_0_, f32[1]{0:T(128)} %copy.18.refs_1_, s32[384,1]{1,0:T(8,128)S(1)} %broadcast_in_dim.15.refs_2_.pos, ...), custom_call_target="tpu_custom_call" | custom-call | flops 2717908992 | bytes 16777216 | tf_op jit(solution)/shard_map/scores/pallas_call | solution.py:114
  51.3 6.6 %scores.3 = (bf16[7,384,384]{2,1,0:T(8,128)(2,1)}, f32[4,384,128]{2,1,0:T(8,128)S(1)}, f32[4,8,384]{2,1,0:T(8,128)S(1)}, bf16[1536,512]{1,0:T(8,128)(2,1)}, bf16[1536,512]{1,0:T(8,128)(2,1)}) custom-call(s32[16]{0:T(128)S(1)} %or_convert_fusion.refs_0_, f32[1]{0:T(128)} %copy.18.refs_1_, s32[384,1]{1,0:T(8,128)S(1)} %broadcast_in_dim.15.refs_2_.pos, ...), custom_call_target="tpu_custom_call" | custom-call | flops 2113929216 | bytes 16777216 | tf_op jit(solution)/shard_map/scores/pallas_call | solution.py:114
  57.9 2.3 %collective-permute-start.11 = (f32[4,384]{1,0:T(4,128)S(1)}, f32[4,384]{1,0:T(4,128)S(1)}, u32[]{:S(2)}, u32[]{:S(2)}) collective-permute-start(f32[4,384]{1,0:T(4,128)S(1)} %add_reduce_fusion.1), channel_id=1, source_target_pairs={{0,12},{4,0},{8,4},{12,8},{1,13},{5,1},{9,5},{13,9},{2,14},{6,2},{... | collective-permute-start | bytes 18440 | tf_op jit(solution)/shard_map/ppermute | solution.py:18
  64.5 3.6 %collective-permute-done.13 = f32[4,384]{1,0:T(4,128)S(1)} collective-permute-done((f32[4,384]{1,0:T(4,128)S(1)}, f32[4,384]{1,0:T(4,128)S(1)}, u32[]{:S(2)}, u32[]{:S(2)}) %collective-permute-start.13) | collective-permute-done | bytes 6176 | tf_op jit(solution)/shard_map/ppermute | solution.py:18
  69.5 3.5 %far_weights.1 = (bf16[384,512]{1,0:T(8,128)(2,1)S(1)}, bf16[384,512]{1,0:T(8,128)(2,1)S(1)}, bf16[384,1536]{1,0:T(8,128)(2,1)S(1)}, bf16[1536,384]{1,0:T(8,128)(2,1)S(1)}) custom-call(f32[4,384,128]{2,1,0:T(8,128)S(1)} %broadcast_in_dim.12.row_inv, f32[4,1,384]{2,1,0:T(1,128)S(1)} %fusion.3.col_inv, bf16[7,384,384]{2,1,0:T(8,128)(2,1)} %get-tuple-element.43.far, ...), custom_call_target="tpu_custom_call" | custom-call | flops 1207959552 | bytes 8388608 | tf_op jit(solution)/shard_map/far_weights/pallas_call | solution.py:213
  73.0 2.4 %collective-permute-start.14 = (bf16[192,512]{1,0:T(8,128)(2,1)S(1)}, bf16[192,512]{1,0:T(8,128)(2,1)S(1)}, u32[]{:S(2)}, u32[]{:S(2)}) collective-permute-start(bf16[192,512]{1,0:T(8,128)(2,1)S(1)} %get-tuple-element.74), channel_id=1, source_target_pairs={{0,3},{1,0},{2,1},{3,2},{4,7},{5,4},{6,5},{7,6},{8,11},{9,8},{10,9... | collective-permute-start | bytes 589832 | tf_op jit(solution)/shard_map/ppermute | solution.py:18
  77.6 7.0 %own_weights.1 = (f32[384,512]{1,0:T(8,128)S(1)}, f32[384,512]{1,0:T(8,128)S(1)}, bf16[1536,1536]{1,0:T(8,128)(2,1)}) custom-call(s32[384,1]{1,0:T(8,128)S(1)} %broadcast_in_dim.15.refs_2_.pos, f32[4,384,128]{2,1,0:T(8,128)S(1)} %broadcast_in_dim.12.row_inv, f32[4,1,384]{2,1,0:T(1,128)S(1)} %fusion.3.col_inv, bf16[9,384,384]{2,1,0:T(8,128)(2,1)} %get-tuple-element.42.near, ...), custom_call_target="tpu_custom_call" | custom-call | flops 1207959552 | bytes 12582912 | tf_op jit(solution)/shard_map/own_weights/pallas_call | solution.py:235
  84.7 4.9 %near_weights.1 = (bf16[384,512]{1,0:T(8,128)(2,1)S(1)}, bf16[384,512]{1,0:T(8,128)(2,1)S(1)}, bf16[384,512]{1,0:T(8,128)(2,1)S(1)}, bf16[384,512]{1,0:T(8,128)(2,1)S(1)}) custom-call(bf16[1536,1536]{1,0:T(8,128)(2,1)} %get-tuple-element.49.weights, bf16[1536,512]{1,0:T(8,128)(2,1)S(1)} %copy-done.1, bf16[1536,512]{1,0:T(8,128)(2,1)S(1)} %copy-done.2, ...), custom_call_target="tpu_custom_call" | custom-call | flops 2415919104 | bytes 12582912 | tf_op jit(solution)/shard_map/near_weights/pallas_call | solution.py:235
  89.6 2.4 %collective-permute-start.20 = (bf16[384,512]{1,0:T(8,128)(2,1)S(1)}, bf16[384,512]{1,0:T(8,128)(2,1)}, u32[]{:S(2)}, u32[]{:S(2)}) collective-permute-start(bf16[384,512]{1,0:T(8,128)(2,1)S(1)} %get-tuple-element.55), channel_id=1, source_target_pairs={{0,12},{4,0},{8,4},{12,8},{1,13},{5,1},{9,5},{13,9},{2,14},{6,2},{... | collective-permute-start | bytes 1179656 | tf_op jit(solution)/shard_map/ppermute | solution.py:18
  92.1 3.2 %collective-permute-start.18 = (bf16[384,512]{1,0:T(8,128)(2,1)S(1)}, bf16[384,512]{1,0:T(8,128)(2,1)}, u32[]{:S(2)}, u32[]{:S(2)}) collective-permute-start(bf16[384,512]{1,0:T(8,128)(2,1)S(1)} %get-tuple-element.52), channel_id=1, source_target_pairs={{0,3},{1,0},{2,1},{3,2},{4,7},{5,4},{6,5},{7,6},{8,11},{9,8},{10,9... | collective-permute-start | bytes 1179656 | tf_op jit(solution)/shard_map/ppermute | solution.py:18
  95.3 5.1 %collective-permute-done.20 = bf16[384,512]{1,0:T(8,128)(2,1)} collective-permute-done((bf16[384,512]{1,0:T(8,128)(2,1)S(1)}, bf16[384,512]{1,0:T(8,128)(2,1)}, u32[]{:S(2)}, u32[]{:S(2)}) %collective-permute-start.20) | collective-permute-done | bytes 393248 | tf_op jit(solution)/shard_map/ppermute | solution.py:18
  100.4 3.4 %collective-permute-done.21 = bf16[384,512]{1,0:T(8,128)(2,1)} collective-permute-done((bf16[384,512]{1,0:T(8,128)(2,1)S(1)}, bf16[384,512]{1,0:T(8,128)(2,1)}, u32[]{:S(2)}, u32[]{:S(2)}) %collective-permute-start.21) | collective-permute-done | bytes 393248 | tf_op jit(solution)/shard_map/ppermute | solution.py:18
  112.9 2.8 %collective-permute-start.27 = (bf16[384,512]{1,0:T(8,128)(2,1)S(1)}, bf16[384,512]{1,0:T(8,128)(2,1)S(1)}, u32[]{:S(2)}, u32[]{:S(2)}) collective-permute-start(bf16[384,512]{1,0:T(8,128)(2,1)S(1)} %collective-permute-done.25.refs_3_), channel_id=1, source_target_pairs={{0,96},{32,0},{64,32},{96,64},{1,97},{33,1},{65,33},{97,65},{2,98}... | collective-permute-start | bytes 1179656 | tf_op jit(solution)/shard_map/ppermute | solution.py:18
  117.7 7.7 %collective-permute-done.31 = f32[8,128]{1,0:T(8,128)S(1)} collective-permute-done((f32[8,128]{1,0:T(8,128)S(1)}, f32[8,128]{1,0:T(8,128)S(1)}, u32[]{:S(2)}, u32[]{:S(2)}) %collective-permute-start.31) | collective-permute-done | bytes 4128 | tf_op jit(solution)/shard_map/ppermute | solution.py:44
  128.6 2.1 %collective-permute-start.29 = (bf16[384,512]{1,0:T(8,128)(2,1)S(1)}, bf16[384,512]{1,0:T(8,128)(2,1)S(1)}, u32[]{:S(2)}, u32[]{:S(2)}) collective-permute-start(bf16[384,512]{1,0:T(8,128)(2,1)S(1)} %collective-permute-done.27.refs_5_), channel_id=1, source_target_pairs={{0,96},{32,0},{64,32},{96,64},{1,97},{33,1},{65,33},{97,65},{2,98}... | collective-permute-start | bytes 1179656 | tf_op jit(solution)/shard_map/ppermute | solution.py:18
  130.7 9.3 %convolution_convert_fusion = bf16[384,3584]{1,0:T(8,128)(2,1)} fusion(bf16[384,1024]{1,0:T(8,128)(2,1)S(1)} %divide_convert_fusion, bf16[3584,1024]{1,0:T(8,128)(2,1)} %param.6), kind=kOutput, calls=%fused_computation | convolution fusion | flops 2819948544 | bytes 10878976 | tf_op jit(solution)/shard_map/dot_general | solution.py:328
  140.6 5.6 %near_rows.1.first = f32[896,512]{1,0:T(8,128)S(1)} custom-call(s32[4]{0:T(128)S(1)} %and_select_fusion.3.places, bf16[4,384,896]{2,1,0:T(8,128)(2,1)} %all-to-all-done.hidden_own, bf16[4,384,896]{2,1,0:T(8,128)(2,1)} %collective-permute-done.22.hidden_other, bf16[384,512]{1,0:T(8,128)(2,1)S(1)} %get-tuple-element.70.refs_0_, ...), custom_call_target="tpu_custom_call" | custom-call | flops 2113929216 | bytes 12582912 | tf_op jit(solution)/shard_map/near_rows/pallas_call | solution.py:235
  152.3 3.8 %last_rows.1 = bf16[32,32,512]{2,1,0:T(8,128)(2,1)S(1)} custom-call(s32[4]{0:T(128)S(1)} %and_select_fusion.3.places, bf16[4,384,896]{2,1,0:T(8,128)(2,1)} %all-to-all-done.hidden_own, bf16[4,384,896]{2,1,0:T(8,128)(2,1)} %collective-permute-done.22.hidden_other, bf16[384,512]{1,0:T(8,128)(2,1)S(1)} %collective-permute-done.28.own, ...), custom_call_target="tpu_custom_call" | custom-call | flops 704643072 | bytes 12582912 | tf_op jit(solution)/shard_map/last_rows/pallas_call | solution.py:235
  156.1 22.2 %all_to_all.10 = bf16[32,32,512]{2,1,0:T(8,128)(2,1)S(1)} all-to-all(bf16[32,32,512]{2,1,0:T(8,128)(2,1)S(1)} %last_rows.1), channel_id=1, replica_groups=mesh['y'=4,'core'=2,'z'=4,'x'=4] {'core','z','x'}, dimensions={0} | all-to-all | bytes 2097152 | tf_op jit(solution)/shard_map/all_to_all | solution.py:363
  (133 shorter events, 46.4 us)
Async XLA Ops:
  7.3 20.5 %collective-permute-start = (bf16[384,1024]{1,0:T(8,128)(2,1)S(1)}, bf16[384,1024]{1,0:T(8,128)(2,1)S(1)}, u32[]{:S(2)}, u32[]{:S(2)}) collective-permute-start(bf16[384,1024]{1,0:T(8,128)(2,1)S(1)} %fusion.13.refs_3_.refs_6_.refs_8_), channel_id=1, source_target_pairs={{0,1},{1,2},{2,3},{3,0},{4,5},{5,6},{6,7},{7,4},{8,9},{9,10},{10,1... | collective-permute-start | bytes 2359304 | tf_op jit(solution)/shard_map/ppermute | solution.py:18
  8.9 20.1 %collective-permute-start.1 = (bf16[384,1024]{1,0:T(8,128)(2,1)S(1)}, bf16[384,1024]{1,0:T(8,128)(2,1)S(1)}, u32[]{:S(2)}, u32[]{:S(2)}) collective-permute-start(bf16[384,1024]{1,0:T(8,128)(2,1)S(1)} %fusion.13.refs_3_.refs_6_.refs_8_), channel_id=1, source_target_pairs={{0,3},{1,0},{2,1},{3,2},{4,7},{5,4},{6,5},{7,6},{8,11},{9,8},{10,9... | collective-permute-start | bytes 2359304 | tf_op jit(solution)/shard_map/ppermute | solution.py:18
  10.6 22.0 %collective-permute-start.2 = (bf16[384,1024]{1,0:T(8,128)(2,1)S(1)}, bf16[384,1024]{1,0:T(8,128)(2,1)S(1)}, u32[]{:S(2)}, u32[]{:S(2)}) collective-permute-start(bf16[384,1024]{1,0:T(8,128)(2,1)S(1)} %fusion.13.refs_3_.refs_6_.refs_8_), channel_id=1, source_target_pairs={{0,4},{4,8},{8,12},{12,0},{1,5},{5,9},{9,13},{13,1},{2,6},{6,10},{... | collective-permute-start | bytes 2359304 | tf_op jit(solution)/shard_map/ppermute | solution.py:18
  12.6 22.9 %collective-permute-start.3 = (bf16[384,1024]{1,0:T(8,128)(2,1)S(1)}, bf16[384,1024]{1,0:T(8,128)(2,1)}, u32[]{:S(2)}, u32[]{:S(2)}) collective-permute-start(bf16[384,1024]{1,0:T(8,128)(2,1)S(1)} %fusion.13.refs_3_.refs_6_.refs_8_), channel_id=1, source_target_pairs={{0,12},{4,0},{8,4},{12,8},{1,13},{5,1},{9,5},{13,9},{2,14},{6,2},{... | collective-permute-start | bytes 2359304 | tf_op jit(solution)/shard_map/ppermute | solution.py:18
  16.7 52.4 %all-to-all-start = ((bf16[4,384,896]{2,1,0:T(8,128)(2,1)}), bf16[4,384,896]{2,1,0:T(8,128)(2,1)}, u32[]{:S(2)}, u32[]{:S(2)}) async-start(bf16[4,384,896]{2,1,0:T(8,128)(2,1)} %pad_maximum_fusion), calls=%async_computation | async-start | bytes 5505024 | tf_op jit(solution)/shard_map/all_to_all | solution.py:273
  28.5 21.6 %collective-permute-start.4 = (bf16[192,1024]{1,0:T(8,128)(2,1)}, bf16[192,1024]{1,0:T(8,128)(2,1)}, u32[]{:S(2)}, u32[]{:S(2)}) collective-permute-start(bf16[192,1024]{1,0:T(8,128)(2,1)} %slice.142), channel_id=1, source_target_pairs={{0,1},{1,2},{2,3},{3,0},{4,5},{5,6},{6,7},{7,4},{8,9},{9,10},{10,1... | collective-permute-start | bytes 1179656 | tf_op jit(solution)/shard_map/ppermute | solution.py:18
  29.8 20.3 %collective-permute-start.5 = (bf16[192,1024]{1,0:T(8,128)(2,1)}, bf16[192,1024]{1,0:T(8,128)(2,1)}, u32[]{:S(2)}, u32[]{:S(2)}) collective-permute-start(bf16[192,1024]{1,0:T(8,128)(2,1)} %slice.143), channel_id=1, source_target_pairs={{0,3},{1,0},{2,1},{3,2},{4,7},{5,4},{6,5},{7,6},{8,11},{9,8},{10,9... | collective-permute-start | bytes 1179656 | tf_op jit(solution)/shard_map/ppermute | solution.py:18
  33.4 16.7 %collective-permute-start.6 = (bf16[192,1024]{1,0:T(8,128)(2,1)}, bf16[192,1024]{1,0:T(8,128)(2,1)}, u32[]{:S(2)}, u32[]{:S(2)}) collective-permute-start(bf16[192,1024]{1,0:T(8,128)(2,1)} %slice.144), channel_id=1, source_target_pairs={{0,4},{4,8},{8,12},{12,0},{1,5},{5,9},{9,13},{13,1},{2,6},{6,10},{... | collective-permute-start | bytes 1179656 | tf_op jit(solution)/shard_map/ppermute | solution.py:18
  37.3 12.8 %collective-permute-start.7 = (bf16[192,1024]{1,0:T(8,128)(2,1)}, bf16[192,1024]{1,0:T(8,128)(2,1)}, u32[]{:S(2)}, u32[]{:S(2)}) collective-permute-start(bf16[192,1024]{1,0:T(8,128)(2,1)} %slice.145), channel_id=1, source_target_pairs={{0,12},{4,0},{8,4},{12,8},{1,13},{5,1},{9,5},{13,9},{2,14},{6,2},{... | collective-permute-start | bytes 1179656 | tf_op jit(solution)/shard_map/ppermute | solution.py:18
  69.4 38.3 %collective-permute-start.22 = (bf16[4,384,896]{2,1,0:T(8,128)(2,1)}, bf16[4,384,896]{2,1,0:T(8,128)(2,1)}, u32[]{:S(2)}, u32[]{:S(2)}) collective-permute-start(bf16[4,384,896]{2,1,0:T(8,128)(2,1)} %all-to-all-done.hidden_own), channel_id=1, source_target_pairs={{0,16},{16,0},{1,17},{17,1},{2,18},{18,2},{3,19},{19,3},{4,20},{20... | collective-permute-start | bytes 8257544 | tf_op jit(solution)/shard_map/ppermute | solution.py:22
  73.0 11.6 %collective-permute-start.14 = (bf16[192,512]{1,0:T(8,128)(2,1)S(1)}, bf16[192,512]{1,0:T(8,128)(2,1)S(1)}, u32[]{:S(2)}, u32[]{:S(2)}) collective-permute-start(bf16[192,512]{1,0:T(8,128)(2,1)S(1)} %get-tuple-element.74), channel_id=1, source_target_pairs={{0,3},{1,0},{2,1},{3,2},{4,7},{5,4},{6,5},{7,6},{8,11},{9,8},{10,9... | collective-permute-start | bytes 589832 | tf_op jit(solution)/shard_map/ppermute | solution.py:18
  75.4 9.2 %collective-permute-start.15 = (bf16[192,512]{1,0:T(8,128)(2,1)S(1)}, bf16[192,512]{1,0:T(8,128)(2,1)S(1)}, u32[]{:S(2)}, u32[]{:S(2)}) collective-permute-start(bf16[192,512]{1,0:T(8,128)(2,1)S(1)} %get-tuple-element.73), channel_id=1, source_target_pairs={{0,1},{1,2},{2,3},{3,0},{4,5},{5,6},{6,7},{7,4},{8,9},{9,10},{10,1... | collective-permute-start | bytes 589832 | tf_op jit(solution)/shard_map/ppermute | solution.py:18
  75.5 9.1 %collective-permute-start.16 = (bf16[192,512]{1,0:T(8,128)(2,1)S(1)}, bf16[192,512]{1,0:T(8,128)(2,1)S(1)}, u32[]{:S(2)}, u32[]{:S(2)}) collective-permute-start(bf16[192,512]{1,0:T(8,128)(2,1)S(1)} %get-tuple-element.72), channel_id=1, source_target_pairs={{0,12},{4,0},{8,4},{12,8},{1,13},{5,1},{9,5},{13,9},{2,14},{6,2},{... | collective-permute-start | bytes 589832 | tf_op jit(solution)/shard_map/ppermute | solution.py:18
  89.6 10.8 %collective-permute-start.20 = (bf16[384,512]{1,0:T(8,128)(2,1)S(1)}, bf16[384,512]{1,0:T(8,128)(2,1)}, u32[]{:S(2)}, u32[]{:S(2)}) collective-permute-start(bf16[384,512]{1,0:T(8,128)(2,1)S(1)} %get-tuple-element.55), channel_id=1, source_target_pairs={{0,12},{4,0},{8,4},{12,8},{1,13},{5,1},{9,5},{13,9},{2,14},{6,2},{... | collective-permute-start | bytes 1179656 | tf_op jit(solution)/shard_map/ppermute | solution.py:18
  92.1 11.7 %collective-permute-start.21 = (bf16[384,512]{1,0:T(8,128)(2,1)S(1)}, bf16[384,512]{1,0:T(8,128)(2,1)}, u32[]{:S(2)}, u32[]{:S(2)}) collective-permute-start(bf16[384,512]{1,0:T(8,128)(2,1)S(1)} %get-tuple-element.56), channel_id=1, source_target_pairs={{0,4},{4,8},{8,12},{12,0},{1,5},{5,9},{9,13},{13,1},{2,6},{6,10},{... | collective-permute-start | bytes 1179656 | tf_op jit(solution)/shard_map/ppermute | solution.py:18
  92.1 13.0 %collective-permute-start.18 = (bf16[384,512]{1,0:T(8,128)(2,1)S(1)}, bf16[384,512]{1,0:T(8,128)(2,1)}, u32[]{:S(2)}, u32[]{:S(2)}) collective-permute-start(bf16[384,512]{1,0:T(8,128)(2,1)S(1)} %get-tuple-element.52), channel_id=1, source_target_pairs={{0,3},{1,0},{2,1},{3,2},{4,7},{5,4},{6,5},{7,6},{8,11},{9,8},{10,9... | collective-permute-start | bytes 1179656 | tf_op jit(solution)/shard_map/ppermute | solution.py:18
  95.3 11.1 %collective-permute-start.19 = (bf16[384,512]{1,0:T(8,128)(2,1)S(1)}, bf16[384,512]{1,0:T(8,128)(2,1)}, u32[]{:S(2)}, u32[]{:S(2)}) collective-permute-start(bf16[384,512]{1,0:T(8,128)(2,1)S(1)} %get-tuple-element.53), channel_id=1, source_target_pairs={{0,1},{1,2},{2,3},{3,0},{4,5},{5,6},{6,7},{7,4},{8,9},{9,10},{10,1... | collective-permute-start | bytes 1179656 | tf_op jit(solution)/shard_map/ppermute | solution.py:18
  112.4 15.0 %collective-permute-start.23 = (bf16[384,512]{1,0:T(8,128)(2,1)S(1)}, bf16[384,512]{1,0:T(8,128)(2,1)S(1)}, u32[]{:S(2)}, u32[]{:S(2)}) collective-permute-start(bf16[384,512]{1,0:T(8,128)(2,1)S(1)} %get-tuple-element.70.refs_0_), channel_id=1, source_target_pairs={{0,32},{32,64},{64,96},{96,0},{1,33},{33,65},{65,97},{97,1},{2,34}... | collective-permute-start | bytes 1179656 | tf_op jit(solution)/shard_map/ppermute | solution.py:18
  112.9 15.7 %collective-permute-start.27 = (bf16[384,512]{1,0:T(8,128)(2,1)S(1)}, bf16[384,512]{1,0:T(8,128)(2,1)S(1)}, u32[]{:S(2)}, u32[]{:S(2)}) collective-permute-start(bf16[384,512]{1,0:T(8,128)(2,1)S(1)} %collective-permute-done.25.refs_3_), channel_id=1, source_target_pairs={{0,96},{32,0},{64,32},{96,64},{1,97},{33,1},{65,33},{97,65},{2,98}... | collective-permute-start | bytes 1179656 | tf_op jit(solution)/shard_map/ppermute | solution.py:18
  115.7 9.7 %collective-permute-start.31 = (f32[8,128]{1,0:T(8,128)S(1)}, f32[8,128]{1,0:T(8,128)S(1)}, u32[]{:S(2)}, u32[]{:S(2)}) collective-permute-start(f32[8,128]{1,0:T(8,128)S(1)} %broadcast_add_fusion), channel_id=1, source_target_pairs={{0,64},{32,96},{64,0},{96,32},{1,65},{33,97},{65,1},{97,33},{2,66}... | collective-permute-start | bytes 12296 | tf_op jit(solution)/shard_map/ppermute | solution.py:44
  125.4 14.6 %collective-permute-start.24 = (bf16[384,512]{1,0:T(8,128)(2,1)S(1)}, bf16[384,512]{1,0:T(8,128)(2,1)S(1)}, u32[]{:S(2)}, u32[]{:S(2)}) collective-permute-start(bf16[384,512]{1,0:T(8,128)(2,1)S(1)} %get-tuple-element.70.refs_0_), channel_id=1, source_target_pairs={{0,96},{32,0},{64,32},{96,64},{1,97},{33,1},{65,33},{97,65},{2,98}... | collective-permute-start | bytes 1179656 | tf_op jit(solution)/shard_map/ppermute | solution.py:18
  127.4 13.3 %collective-permute-start.26 = (bf16[384,512]{1,0:T(8,128)(2,1)S(1)}, bf16[384,512]{1,0:T(8,128)(2,1)S(1)}, u32[]{:S(2)}, u32[]{:S(2)}) collective-permute-start(bf16[384,512]{1,0:T(8,128)(2,1)S(1)} %collective-permute-done.25.refs_3_), channel_id=1, source_target_pairs={{0,32},{32,64},{64,96},{96,0},{1,33},{33,65},{65,97},{97,1},{2,34}... | collective-permute-start | bytes 1179656 | tf_op jit(solution)/shard_map/ppermute | solution.py:18
  127.4 19.3 %collective-permute-start.28 = (bf16[384,512]{1,0:T(8,128)(2,1)S(1)}, bf16[384,512]{1,0:T(8,128)(2,1)S(1)}, u32[]{:S(2)}, u32[]{:S(2)}) collective-permute-start(bf16[384,512]{1,0:T(8,128)(2,1)S(1)} %collective-permute-done.23.refs_1_), channel_id=1, source_target_pairs={{0,32},{32,64},{64,96},{96,0},{1,33},{33,65},{65,97},{97,1},{2,34}... | collective-permute-start | bytes 1179656 | tf_op jit(solution)/shard_map/ppermute | solution.py:18
  128.6 18.2 %collective-permute-start.29 = (bf16[384,512]{1,0:T(8,128)(2,1)S(1)}, bf16[384,512]{1,0:T(8,128)(2,1)S(1)}, u32[]{:S(2)}, u32[]{:S(2)}) collective-permute-start(bf16[384,512]{1,0:T(8,128)(2,1)S(1)} %collective-permute-done.27.refs_5_), channel_id=1, source_target_pairs={{0,96},{32,0},{64,32},{96,64},{1,97},{33,1},{65,33},{97,65},{2,98}... | collective-permute-start | bytes 1179656 | tf_op jit(solution)/shard_map/ppermute | solution.py:18
  (22 other events, 131.5 us)
where the time goes:
time: 182 us
  starting transfers between devices  48.5 us (27%)
  Pallas kernels  38.3 us (21%)
  waiting for transfers between devices  28.5 us (16%)
  blocking collectives  22.2 us (12%)
  matrix products  15.7 us (9%)
  other arithmetic  11.3 us (6%)
  local copies, waits for them, and re-layouts  8.54 us (5%)
  between operations  8.41 us (5%)
    ppermute x28, starting transfers between devices, send(): return lax.ppermute(array, axis, [(i, (i + step) % 4) for i in range(4)])  39.8 us
    all_to_all x1, blocking collectives, per_device(): arrived = lax.all_to_all(part, ('core', 'z', 'x'), 0, 0).astype(jnp.float32)  22.2 us
    pallas_call x4, Pallas kernels, call(): pl.pallas_call(kernel, out_shape=out_shape, in_specs=[smem] * scalars + [...  21.4 us
    ppermute x28, waiting for transfers between devices, send(): return lax.ppermute(array, axis, [(i, (i + step) % 4) for i in range(4)])  20.8 us
    pallas_call x2, Pallas kernels, score_tiles(): pl.pallas_call(functools.partial(score_kernel, tiles, names, pieces, fina...  13.4 us
    dot_general x1, matrix products, per_device(): lax.dot_general(grad_projected, projection, (((1,), (1,)), ((), ())), pre...  9.33 us
    ppermute x2, waiting for transfers between devices, total_over_y(): value = value + lax.ppermute(value, 'y', [(i, i ^ bit) for i in range(4)])  7.75 us
    dot_general x1, matrix products, per_device(): projected = jnp.dot(hidden, projection, preferred_element_type=jnp.float32)  6.39 us
  transfers between devices with their start and end apart: 33, of which 10 were waited for; matrix products, arithmetic and copies ran while one was open for 12% of the time, Pallas kernels for 19%

commit v1 on v0

v1 whole, which is shorter than its diff:
```python
import functools

import jax
import jax.numpy as jnp
from jax import lax
from jax.experimental import pallas as pl
from jax.experimental.pallas import tpu as pltpu
from jax.sharding import Mesh, PartitionSpec as P

epsilon = 1e-06
shift = 3.0
AXES = ("y", "core", "z", "x")
ORDER = (0, 1, 3, 2)
NEAR = [(0, 0), (0, 1), (0, 3), (1, 0), (1, 1), (1, 3), (3, 0), (3, 1), (3, 3)]
FAR = [(0, 2), (1, 2), (3, 2), (2, 0), (2, 1), (2, 2), (2, 3)]


def send(array, axis, step):
    return lax.ppermute(array, axis, [(i, (i + step) % 4) for i in range(4)])


def swap(array):
    return lax.ppermute(array, "core", [(0, 1), (1, 0)])


def ring_gather(block, axis):
    half = block.shape[0] // 2
    back = send(block, axis, 1)
    ahead = send(block, axis, -1)
    far_top = send(back[:half], axis, 1)
    far_bottom = send(ahead[half:], axis, -1)
    return (back,), (far_top, far_bottom), (ahead,)


def ring_total(parts, axis):
    total = parts
    for d in (1, 2, 3):
        seen = send(parts, axis, -d)
        total = total + jnp.roll(seen, -d, axis=0)
    return total


def target_of(pos):
    rows = pos.shape[0]
    return lax.broadcasted_iota(jnp.int32, (rows, rows), 1) == pos


def score_kernel(tiles, names, pieces, final, *refs):
    active, scale, pos = refs[:3]
    count = sum(pieces)
    outs = refs[3 + 2 * count :]
    powers, row_sums, col_sums = outs[:3]
    rows = pos.shape[0]
    row_sums[...] = jnp.zeros_like(row_sums)
    col_sums[...] = jnp.zeros_like(col_sums)
    if final:
        outs[5][...] = jnp.zeros_like(outs[5])
    joined = list(outs[6:])
    row_units, col_units = [], []
    for refs_in, units in ((refs[3 : 3 + count], row_units), (refs[3 + count : 3 + 2 * count], col_units)):
        at = 0
        for many in pieces:
            source = refs_in[at]
            if many > 1:
                source = joined.pop()
                cut = rows // many
                for part in range(many):
                    source[cut * part : cut * (part + 1)] = refs_in[at + part][...]
            units.append(source)
            at += many
    factor = scale[0]
    for place, (dx, dz) in enumerate(tiles):
        scores = factor * lax.dot_general(
            row_units[names.index(dx)][...],
            col_units[names.index(dz)][...],
            (((1,), (1,)), ((), ())),
            preferred_element_type=jnp.float32,
        )
        power = jnp.exp(scores - shift)
        if (dx, dz) == (0, 0):
            here = lax.broadcasted_iota(jnp.int32, (rows, rows), 0)
            there = lax.broadcasted_iota(jnp.int32, (rows, rows), 1)
            power = jnp.where(here == there, 0.0, power)
            hit = jnp.where(target_of(pos[...]), scores, 0.0)
            outs[5][...] = hit[:, :128] + hit[:, 128:256] + hit[:, 256:]
        else:
            power = power * active[4 * dx + dz]
        powers[place] = power.astype(jnp.bfloat16)
        row_sums[dx] += power[:, :128] + power[:, 128:256] + power[:, 256:]
        col_sums[dz] += jnp.sum(power.reshape(rows // 8, 8, rows), axis=0)
    half = row_units[0].shape[1] // 2
    for place, d in enumerate([2] if final else names):
        outs[3][rows * place : rows * (place + 1)] = row_units[names.index(d)][:, half:]
        outs[4][rows * place : rows * (place + 1)] = col_units[names.index(d)][:, :half]


def score_tiles(tiles, final, active, scale, pos, row_pieces, col_pieces):
    names = sorted({d for tile in tiles for d in tile})
    rows = pos.shape[0]
    width = row_pieces[0][0].shape[1]
    smem = pl.BlockSpec(memory_space=pltpu.SMEM)
    vmem = pl.BlockSpec(memory_space=pltpu.VMEM)
    out_shape = [
        jax.ShapeDtypeStruct((len(tiles), rows, rows), jnp.bfloat16),
        jax.ShapeDtypeStruct((4, rows, 128), jnp.float32),
        jax.ShapeDtypeStruct((4, 8, rows), jnp.float32),
    ]
    out_shape += [jax.ShapeDtypeStruct(((1 if final else 3) * rows, width // 2), jnp.bfloat16)] * 2
    out_shape += [jax.ShapeDtypeStruct((8 if final else rows, 128), jnp.float32)]
    scratch = [pltpu.VMEM((rows, width), jnp.bfloat16)] * 2 if final else []
    pieces = [len(row_pieces[d]) for d in names]
    return pl.pallas_call(
        functools.partial(score_kernel, tiles, names, pieces, final),
        out_shape=tuple(out_shape),
        in_specs=[smem, smem] + [vmem] * (1 + 2 * sum(pieces)),
        out_specs=(vmem,) * len(out_shape),
        scratch_shapes=scratch,
        compiler_params=pltpu.CompilerParams(vmem_limit_bytes=48 << 20),
        cost_estimate=pl.CostEstimate(
            flops=len(tiles) * 2 * rows * rows * width,
            transcendentals=len(tiles) * rows * rows,
            bytes_accessed=16 << 20,
        ),
        name="scores",
    )(
        active, scale, pos,
        *[piece for d in names for piece in row_pieces[d]],
        *[piece for d in names for piece in col_pieces[d]],
    )


def weight_tile(source, place, dx, dz, row_inv, col_inv):
    inv = row_inv[dx]
    return source[place].astype(jnp.float32) * (jnp.concatenate([inv, inv, inv], axis=1) + col_inv[dz])


def product(left, right):
    return jnp.dot(left, right, preferred_element_type=jnp.float32)


def product_over_rows(left, right):
    return lax.dot_general(left, right, (((0,), (0,)), ((), ())), preferred_element_type=jnp.float32)


def far_kernel(row_inv, col_inv, far, rows_near, rows_far, cols_near, cols_far, far_row, far_col, wide, tall):
    rows = far.shape[1]
    for place, (dx, dz) in enumerate(FAR):
        weight = weight_tile(far, place, dx, dz, row_inv, col_inv).astype(jnp.bfloat16)
        if dx == 2:
            at = rows * ORDER.index(dz)
            wide[:, at : at + rows] = weight
        if dz == 2:
            at = rows * ORDER.index(dx)
            tall[at : at + rows] = weight
    by_row = product(wide[:, : 3 * rows], cols_near[...]) + product(wide[:, 3 * rows :], cols_far[...])
    by_col = product_over_rows(tall[: 3 * rows], rows_near[...]) + product_over_rows(tall[3 * rows :], rows_far[...])
    far_row[...] = by_row.astype(far_row.dtype)
    far_col[...] = by_col.astype(far_col.dtype)


def both_ways(d, weights, wide, tall, rows_near, rows_far, cols_near, cols_far):
    rows = wide.shape[0]
    span = slice(rows * ORDER.index(d), rows * (ORDER.index(d) + 1))
    by_row = product(weights[span], cols_near[...]) + product(tall[span], cols_far[...])
    by_col = product_over_rows(weights[:, span], rows_near[...]) + product_over_rows(wide[:, span], rows_far[...])
    return by_row, by_col


def own_kernel(*refs):
    by_row, by_col = both_ways(0, *refs[:7])
    refs[9][...] = by_row + refs[7][...].astype(jnp.float32)
    refs[10][...] = by_col + refs[8][...].astype(jnp.float32)


def near_kernel(pos, row_inv, col_inv, near, wide, tall, *refs):
    units, outs, weights = refs[:4], refs[4:8], refs[8]
    rows = pos.shape[0]
    for place, (dx, dz) in enumerate(NEAR):
        weight = weight_tile(near, place, dx, dz, row_inv, col_inv)
        if (dx, dz) == (0, 0):
            weight = weight - jnp.where(target_of(pos[...]), 2.0, 0.0)
        row, col = rows * ORDER.index(dx), rows * ORDER.index(dz)
        weights[row : row + rows, col : col + rows] = weight.astype(jnp.bfloat16)
    for place, d in enumerate((1, 3)):
        by_row, by_col = both_ways(d, weights, wide, tall, *units)
        outs[place][...] = by_row.astype(outs[place].dtype)
        outs[2 + place][...] = by_col.astype(outs[2 + place].dtype)


def split_value(value):
    high = value.astype(jnp.bfloat16).astype(jnp.float32)
    middle = (value - high).astype(jnp.bfloat16).astype(jnp.float32)
    low = value - high - middle
    row = lax.broadcasted_iota(jnp.int32, value.shape, 0)
    parts = jnp.where(row == 0, high, jnp.where(row == 1, middle, jnp.where(row == 2, low, 0.0)))
    return parts.astype(jnp.bfloat16)


def row_kernel(scale, core, ring_loss, by_row, by_col, *refs):
    arrivals, (unit_rows, lengths, whole, kept, other) = refs[:4], refs[4:]
    rows, half = by_row.shape
    left, right = by_row[...], by_col[...]
    for seen in arrivals[:2]:
        left = left + seen[...].astype(jnp.float32)
    for seen in arrivals[2:]:
        right = right + seen[...].astype(jnp.float32)
    left, right = scale[0] * left, scale[0] * right
    unit_left, unit_right = unit_rows[:, :half], unit_rows[:, half:]
    along = jnp.sum(unit_left * left, axis=1, keepdims=True) + jnp.sum(unit_right * right, axis=1, keepdims=True)
    length = lengths[...]
    left = ((left - unit_left * along) / length).astype(jnp.bfloat16)
    right = ((right - unit_right * along) / length).astype(jnp.bfloat16)
    whole[:, :half], whole[:, half:] = left, right
    kept[rows:] = split_value(jnp.full((16, half), ring_loss[0], jnp.float32))

    @pl.when(core[0] == 0)
    def _():
        kept[:rows], other[...] = left, right

    @pl.when(core[0] == 1)
    def _():
        kept[:rows], other[...] = right, left


def hidden_kernel(rows, weights, out):
    out[...] = lax.dot_general(
        rows[...], weights[...], (((1,), (1,)), ((), ())), preferred_element_type=jnp.float32
    ).astype(out.dtype)


def hidden_grad(rows, projection, steps=7):
    count, width = rows.shape
    depth = projection.shape[0]
    block = depth // steps
    return pl.pallas_call(
        hidden_kernel,
        grid=(steps,),
        out_shape=jax.ShapeDtypeStruct((count, depth), jnp.bfloat16),
        in_specs=[
            pl.BlockSpec((count, width), lambda i: (0, 0)),
            pl.BlockSpec((block, width), lambda i: (i, 0)),
        ],
        out_specs=pl.BlockSpec((count, block), lambda i: (0, i)),
        compiler_params=pltpu.CompilerParams(vmem_limit_bytes=48 << 20),
        cost_estimate=pl.CostEstimate(
            flops=2 * count * width * depth, transcendentals=0, bytes_accessed=11 << 20
        ),
        name="hidden_grad",
    )(rows, projection)


def gather_kernel(places, hidden_own, hidden_other, *refs):
    pairs, out = refs[:3], refs[3]
    rows = hidden_own.shape[1]
    step = pl.program_id(0)
    for k in range(3):
        @pl.when(step == k)
        def _():
            made = product_over_rows(hidden_own[0], pairs[k][:rows])
            made = made + product_over_rows(hidden_other[0], pairs[k][rows + 16 :])
            if k == 0:
                out[...] = made
            else:
                out[...] += made


def last_kernel(places, hidden_own, hidden_other, own, other, pair, back, ahead, first, out, total):
    rows = other.shape[0]
    total[...] = (
        first[...]
        + product_over_rows(hidden_own[0], own[:rows])
        + product_over_rows(hidden_other[0], other[...])
    )
    loss = jnp.zeros((1, own.shape[1]), jnp.float32)
    for source in (own, pair, back, ahead):
        loss = loss + jnp.sum(source[rows : rows + 16].astype(jnp.float32), axis=0, keepdims=True)
    spare = split_value(jnp.broadcast_to(loss, (16, own.shape[1])))[:4]
    count, padded = out.shape[:2]
    size = padded - 4
    for k in range(count):
        out[k, :size] = total[size * k : size * (k + 1)].astype(out.dtype)
        out[k, size:] = spare


def call_by_place(kernel, name, flops, places, hidden_own, hidden_other, inputs, out_shape, scratch=()):
    block = pl.BlockSpec((1,) + hidden_own.shape[1:], lambda i, places: (places[i], 0, 0))
    def all_of(shape):
        return pl.BlockSpec(shape, lambda i, places: (0,) * len(shape))
    return pl.pallas_call(
        kernel,
        out_shape=out_shape,
        grid_spec=pltpu.PrefetchScalarGridSpec(
            num_scalar_prefetch=1,
            grid=places.shape,
            in_specs=[block, block] + [all_of(array.shape) for array in inputs],
            out_specs=all_of(out_shape.shape),
            scratch_shapes=scratch,
        ),
        compiler_params=pltpu.CompilerParams(vmem_limit_bytes=48 << 20),
        cost_estimate=pl.CostEstimate(flops=flops, transcendentals=0, bytes_accessed=8 << 20),
        name=name,
    )(places, hidden_own, hidden_other, *inputs)


def call(kernel, name, flops, inputs, out_shape, scratch=(), scalars=0):
    vmem = pl.BlockSpec(memory_space=pltpu.VMEM)
    smem = pl.BlockSpec(memory_space=pltpu.SMEM)
    many = isinstance(out_shape, tuple)
    return pl.pallas_call(
        kernel,
        out_shape=out_shape,
        in_specs=[smem] * scalars + [vmem] * (len(inputs) - scalars),
        out_specs=(vmem,) * len(out_shape) if many else vmem,
        scratch_shapes=scratch,
        compiler_params=pltpu.CompilerParams(vmem_limit_bytes=48 << 20),
        cost_estimate=pl.CostEstimate(flops=flops, transcendentals=0, bytes_accessed=12 << 20),
        name=name,
    )(*inputs)


def per_device(hidden, projection, inv_temp, partners, positives):
    rows = hidden.shape[0]
    width = projection.shape[1]
    half = width // 2
    iy, ic = lax.axis_index("y"), lax.axis_index("core")
    iz, ix = lax.axis_index("z"), lax.axis_index("x")
    mine = iz * 4 + ix

    offsets = (partners[0] % 16) ^ mine
    back = jnp.arange(4)
    row_ids = iz * 4 + (ix - back) % 4
    col_ids = ((iz - back) % 4) * 4 + ix
    apart = (row_ids[:, None] ^ col_ids[None, :]).reshape(16)
    active = (jnp.any(apart[:, None] == offsets[None, :], axis=1) | (apart == 0)).astype(jnp.int32)
    pos = (positives % rows)[:, None]

    projected = jnp.dot(hidden, projection, preferred_element_type=jnp.float32)
    lengths = jnp.sqrt(jnp.sum(projected * projected, axis=1, keepdims=True) + epsilon)
    unit_rows = projected / lengths
    unit_low = unit_rows.astype(jnp.bfloat16)

    x_back, x_far, x_ahead = ring_gather(unit_low, "x")
    z_back, z_far, z_ahead = ring_gather(unit_low, "z")

    fourth = hidden.shape[1] // 4
    by_y = jnp.stack([hidden[:, fourth * k : fourth * (k + 1)] for k in range(4)])
    own_hidden = lax.all_to_all(by_y, "y", 0, 0)

    own = (unit_low,)
    near, near_rows, near_cols, rows_near, cols_near, hits = score_tiles(
        NEAR, False, active, inv_temp, pos, {0: own, 1: x_back, 3: x_ahead}, {0: own, 1: z_back, 3: z_ahead}
    )
    far, far_rows, far_cols, rows_far, cols_far, _ = score_tiles(
        FAR,
        True,
        active,
        inv_temp,
        pos,
        {0: own, 1: x_back, 2: x_far, 3: x_ahead},
        {0: own, 1: z_back, 2: z_far, 3: z_ahead},
    )

    row_sums = jnp.sum(near_rows + far_rows, axis=2)
    hit_sum = jnp.full((4, 128), jnp.sum(hits)) * (back == 0)[:, None]
    row_totals = ring_total(jnp.concatenate([row_sums, hit_sum], axis=1), "x")
    row_totals, hit_sum = row_totals[:, :rows], row_totals[:, rows]
    col_totals = ring_total(jnp.sum(near_cols + far_cols, axis=1), "z")
    row_inv = jnp.broadcast_to((1.0 / row_totals)[:, :, None], (4, rows, 128))
    col_inv = (1.0 / col_totals)[:, None, :]
    row_inv, col_inv, own_hidden = lax.optimization_barrier((row_inv, col_inv, own_hidden))
    other_hidden = swap(own_hidden)

    unit = 2 * rows * rows * half
    chunk = jax.ShapeDtypeStruct((rows, half), jnp.float32)
    low_chunk = jax.ShapeDtypeStruct((rows, half), jnp.bfloat16)
    units = (rows_near, rows_far, cols_near, cols_far)
    far_row, far_col, wide, tall = call(
        far_kernel, "far_weights", 8 * unit, (row_inv, col_inv, far, *units),
        (
            low_chunk,
            low_chunk,
            jax.ShapeDtypeStruct((rows, 4 * rows), jnp.bfloat16),
            jax.ShapeDtypeStruct((4 * rows, rows), jnp.bfloat16),
        ),
    )
    x_far_seen, z_far_seen = send(far_row, "x", 2), send(far_col, "z", 2)
    x_next, x_last, z_next, z_last, weights = call(
        near_kernel, "near_weights", 24 * unit, (pos, row_inv, col_inv, near, wide, tall, *units),
        (low_chunk,) * 4 + (jax.ShapeDtypeStruct((3 * rows, 3 * rows), jnp.bfloat16),),
    )
    arrivals = (send(x_next, "x", -1), send(x_last, "x", 1), send(z_next, "z", -1), send(z_last, "z", 1))
    by_row, by_col = call(own_kernel, "own_weights", 8 * unit, (weights, wide, tall, *units, x_far_seen, z_far_seen), (chunk, chunk))
    ring_loss = jnp.sum(shift + jnp.log(row_totals)) - jnp.sum(hit_sum)
    arrivals, other_hidden, ring_loss = lax.optimization_barrier((arrivals, other_hidden, ring_loss))
    grad_projected, kept, other = call(
        row_kernel, "row_gradients", unit,
        (inv_temp, ic[None], ring_loss[None], by_row, by_col, *arrivals, unit_rows, lengths),
        (
            jax.ShapeDtypeStruct((rows, width), jnp.bfloat16),
            jax.ShapeDtypeStruct((rows + 16, half), jnp.bfloat16),
            low_chunk,
        ),
        scalars=3,
    )
    pair = jnp.concatenate([kept, swap(other)], axis=0)
    grad_hidden = hidden_grad(grad_projected, projection)
    pair_back, pair_ahead = send(pair, "y", 1), send(pair, "y", -1)
    own_far = send(pair_back[: rows + 16], "y", 1)
    other_far = send(pair_ahead[rows + 16 :], "y", -1)
    step = 2 * rows * fourth * half
    first = call_by_place(
        gather_kernel, "near_rows", 60 * step, jnp.stack([iy, (iy + 3) % 4, (iy + 1) % 4]),
        own_hidden, other_hidden, (pair, pair_back, pair_ahead),
        jax.ShapeDtypeStruct((fourth, half), jnp.float32),
    )
    first, own_far, other_far, grad_hidden = lax.optimization_barrier((first, own_far, other_far, grad_hidden))
    part = call_by_place(
        last_kernel, "last_rows", 2 * step, ((iy + 2) % 4)[None], own_hidden, other_hidden,
        (own_far, other_far, pair, pair_back, pair_ahead, first),
        jax.ShapeDtypeStruct((32, fourth // 32 + 4, half), jnp.bfloat16),
        scratch=[pltpu.VMEM((fourth, half), jnp.float32)],
    )
    arrived = lax.all_to_all(part, ("core", "z", "x"), 0, 0).astype(jnp.float32)
    sums = jnp.sum(arrived.reshape(2, 16, fourth // 32 + 4, half), axis=1)
    grad_proj = jnp.concatenate([sums[0, : fourth // 32], sums[1, : fourth // 32]], axis=1)
    loss = jnp.sum(sums[:, fourth // 32 :, 0]) / (4 * 128 * rows)
    return (loss, grad_hidden, grad_proj)


def solution(mesh):
    split = Mesh(mesh.devices.reshape(4, 2, 4, 4), AXES)
    return jax.shard_map(
        per_device,
        mesh=split,
        in_specs=(P(AXES, None), P(), P(), P(AXES, None), P(AXES)),
        out_specs=(P(), P(AXES, None), P(AXES, None)),
        check_vma=False,
    )
```

time: 182 us -> 169 us (0.929)
  Pallas kernels: 38.3 us -> 48 us
  matrix products: 15.7 us -> 6.26 us
  starting transfers between devices: 48.5 us -> 39.8 us
  between operations: 8.41 us -> 4.74 us
  other arithmetic: 11.3 us -> 7.9 us
  local copies, waits for them, and re-layouts: 8.54 us -> 11.5 us
    pallas_call x1 -> x3, Pallas kernels: 3.48 us -> 16.6 us  [the longest x1 8.58 us: hidden_grad(): pl.pallas_call(hidden_kernel, grid=(steps,), out_shape=jax.ShapeDtypeStru...]
    dot_general x1 -> x0, matrix products: 9.33 us -> none  [per_device(): lax.dot_general(grad_projected, projection, (((1,), (1,)), ((), ())), pre...]
    ppermute x2 -> x0, waiting for transfers between devices: 7.75 us -> none  [total_over_y(): value = value + lax.ppermute(value, 'y', [(i, i ^ bit) for i in range(4)])]
    ppermute x28 -> x24, waiting for transfers between devices: 20.8 us -> 27.4 us  [send(): return lax.ppermute(array, axis, [(i, (i + step) % 4) for i in range(4)])]
    ppermute x28 -> x24, starting transfers between devices: 39.8 us -> 34.9 us  [send(): return lax.ppermute(array, axis, [(i, (i + step) % 4) for i in range(4)])]
    pallas_call x4, Pallas kernels: 21.4 us -> 17.3 us  [call(): pl.pallas_call(kernel, out_shape=out_shape, in_specs=[smem] * scalars + [...]
    ppermute x2 -> x0, starting transfers between devices: 3.85 us -> none  [total_over_y(): value = value + lax.ppermute(value, 'y', [(i, i ^ bit) for i in range(4)])]
    unnamed x26 -> x35, local copies, waits for them, and re-layouts: 2.92 us -> 6.26 us
  transfers between devices with their start and end apart: 33 -> 27, of which waited for: 10 -> 10; matrix products, arithmetic and copies ran while one was open for 12% -> 6% of each run, Pallas kernels for 19% -> 26%
where the time goes in v1:
time: 169 us; the launch traced here: 168 us
  Pallas kernels  48 us (28%)
  starting transfers between devices  39.8 us (24%)
  waiting for transfers between devices  29.1 us (17%)
  blocking collectives  20.8 us (12%)
  local copies, waits for them, and re-layouts  11.5 us (7%)
  other arithmetic  7.9 us (5%)
  matrix products  6.26 us (4%)
  between operations  4.74 us (3%)
    ppermute x24, starting transfers between devices, send(): return lax.ppermute(array, axis, [(i, (i + step) % 4) for i in range(4)])  34.9 us
    ppermute x24, waiting for transfers between devices, send(): return lax.ppermute(array, axis, [(i, (i + step) % 4) for i in range(4)])  27.4 us
    all_to_all x1, blocking collectives, per_device(): arrived = lax.all_to_all(part, ('core', 'z', 'x'), 0, 0).astype(jnp.float32)  20.8 us
    pallas_call x4, Pallas kernels, call(): pl.pallas_call(kernel, out_shape=out_shape, in_specs=[smem] * scalars + [...  17.3 us
    pallas_call x2, Pallas kernels, score_tiles(): pl.pallas_call(functools.partial(score_kernel, tiles, names, pieces, fina...  14.2 us
    pallas_call x1, Pallas kernels, hidden_grad(): pl.pallas_call(hidden_kernel, grid=(steps,), out_shape=jax.ShapeDtypeStru...  8.58 us
    pallas_call x2, Pallas kernels, call_by_place(): pl.pallas_call(kernel, out_shape=out_shape, grid_spec=pltpu.PrefetchScala...  7.99 us
    unnamed x35, local copies, waits for them, and re-layouts  6.26 us
  transfers between devices with their start and end apart: 27, of which 10 were waited for; matrix products, arithmetic and copies ran while one was open for 6% of the time, Pallas kernels for 26%

profile of v1, /device:TPU:0, one launch (start us, length us, event | category | flops | bytes accessed | tf_op | source)
XLA Modules:
  0.0 168.0 jit_solution(4657835662559419985)
XLA Ops:
  0.6 6.3 %multiply_reduce_fusion = (f32[384]{0:T(512)S(1)}, f32[384,1024]{1,0:T(8,128)S(1)}) fusion(bf16[384,3584]{1,0:T(8,128)(2,1)} %param.5, bf16[3584,1024]{1,0:T(8,128)(2,1)} %weights.1), kind=kOutput, calls=%fused_computation.2 | convolution fusion | flops 2819358208 | bytes 11666944 | tf_op jit(solution)/shard_map/dot_general | solution.py:337
  11.6 2.0 %collective-permute-start.2 = (bf16[384,1024]{1,0:T(8,128)(2,1)S(1)}, bf16[384,1024]{1,0:T(8,128)(2,1)S(1)}, u32[]{:S(2)}, u32[]{:S(2)}) collective-permute-start(bf16[384,1024]{1,0:T(8,128)(2,1)S(1)} %get-tuple-element.79.refs_3_.refs_6_.refs_8_), channel_id=1, source_target_pairs={{0,4},{4,8},{8,12},{12,0},{1,5},{5,9},{9,13},{13,1},{2,6},{6,10},{... | collective-permute-start | bytes 2359304 | tf_op jit(solution)/shard_map/ppermute | solution.py:19
  13.6 2.1 %collective-permute-start.3 = (bf16[384,1024]{1,0:T(8,128)(2,1)S(1)}, bf16[384,1024]{1,0:T(8,128)(2,1)}, u32[]{:S(2)}, u32[]{:S(2)}) collective-permute-start(bf16[384,1024]{1,0:T(8,128)(2,1)S(1)} %get-tuple-element.79.refs_3_.refs_6_.refs_8_), channel_id=1, source_target_pairs={{0,12},{4,0},{8,4},{12,8},{1,13},{5,1},{9,5},{13,9},{2,14},{6,2},{... | collective-permute-start | bytes 2359304 | tf_op jit(solution)/shard_map/ppermute | solution.py:19
  17.7 4.7 %all-to-all-start = ((bf16[4,384,896]{2,1,0:T(8,128)(2,1)}), bf16[4,384,896]{2,1,0:T(8,128)(2,1)}, u32[]{:S(2)}, u32[]{:S(2)}) async-start(bf16[4,384,896]{2,1,0:T(8,128)(2,1)} %pad_maximum_fusion), calls=%async_computation | async-start | bytes 5505024 | tf_op jit(solution)/shard_map/all_to_all | solution.py:347
  22.9 5.9 %collective-permute-done.refs_4_ = bf16[384,1024]{1,0:T(8,128)(2,1)S(1)} collective-permute-done((bf16[384,1024]{1,0:T(8,128)(2,1)S(1)}, bf16[384,1024]{1,0:T(8,128)(2,1)S(1)}, u32[]{:S(2)}, u32[]{:S(2)}) %collective-permute-start) | collective-permute-done | bytes 786464 | tf_op jit(solution)/shard_map/ppermute | solution.py:19
  30.9 2.8 %collective-permute-start.5 = (bf16[192,1024]{1,0:T(8,128)(2,1)}, bf16[192,1024]{1,0:T(8,128)(2,1)}, u32[]{:S(2)}, u32[]{:S(2)}) collective-permute-start(bf16[192,1024]{1,0:T(8,128)(2,1)} %slice.121), channel_id=1, source_target_pairs={{0,3},{1,0},{2,1},{3,2},{4,7},{5,4},{6,5},{7,6},{8,11},{9,8},{10,9... | collective-permute-start | bytes 1179656 | tf_op jit(solution)/shard_map/ppermute | solution.py:19
  34.5 2.1 %collective-permute-start.6 = (bf16[192,1024]{1,0:T(8,128)(2,1)}, bf16[192,1024]{1,0:T(8,128)(2,1)}, u32[]{:S(2)}, u32[]{:S(2)}) collective-permute-start(bf16[192,1024]{1,0:T(8,128)(2,1)} %slice.122), channel_id=1, source_target_pairs={{0,4},{4,8},{8,12},{12,0},{1,5},{5,9},{9,13},{13,1},{2,6},{6,10},{... | collective-permute-start | bytes 1179656 | tf_op jit(solution)/shard_map/ppermute | solution.py:19
  38.4 2.1 %collective-permute-start.7 = (bf16[192,1024]{1,0:T(8,128)(2,1)}, bf16[192,1024]{1,0:T(8,128)(2,1)}, u32[]{:S(2)}, u32[]{:S(2)}) collective-permute-start(bf16[192,1024]{1,0:T(8,128)(2,1)} %slice.123), channel_id=1, source_target_pairs={{0,12},{4,0},{8,4},{12,8},{1,13},{5,1},{9,5},{13,9},{2,14},{6,2},{... | collective-permute-start | bytes 1179656 | tf_op jit(solution)/shard_map/ppermute | solution.py:19
  42.4 7.7 %scores.2 = (bf16[9,384,384]{2,1,0:T(8,128)(2,1)}, f32[4,384,128]{2,1,0:T(8,128)S(1)}, f32[4,8,384]{2,1,0:T(8,128)S(1)}, bf16[1152,512]{1,0:T(8,128)(2,1)}, bf16...) custom-call(s32[16]{0:T(128)S(1)} %or_convert_fusion.refs_0_, f32[1]{0:T(128)S(6)} %copy.21.refs_1_.scale, ...), custom_call_target="tpu_custom_call" | custom-call | flops 2717908992 | bytes 16777216 | tf_op jit(solution)/shard_map/scores/pallas_call | solution.py:112
  53.6 6.4 %scores.3 = (bf16[7,384,384]{2,1,0:T(8,128)(2,1)}, f32[4,384,128]{2,1,0:T(8,128)S(1)}, f32[4,8,384]{2,1,0:T(8,128)S(1)}, bf16[384,512]{1,0:T(8,128)(2,1)S(1)}, b...) custom-call(s32[16]{0:T(128)S(1)} %or_convert_fusion.refs_0_, f32[1]{0:T(128)S(6)} %copy.21.refs_1_.scale, ...), custom_call_target="tpu_custom_call" | custom-call | flops 2113929216 | bytes 16777216 | tf_op jit(solution)/shard_map/scores/pallas_call | solution.py:112
  60.0 2.1 %collective-permute-start.12 = (f32[4,384]{1,0:T(4,128)S(1)}, f32[4,384]{1,0:T(4,128)S(1)}, u32[]{:S(2)}, u32[]{:S(2)}) collective-permute-start(f32[4,384]{1,0:T(4,128)S(1)} %add_reduce_fusion.1), channel_id=1, source_target_pairs={{0,8},{4,12},{8,0},{12,4},{1,9},{5,13},{9,1},{13,5},{2,10},{6,14},... | collective-permute-start | bytes 18440 | tf_op jit(solution)/shard_map/ppermute | solution.py:19
  68.9 2.4 %collective-permute-done.10 = f32[4,512]{1,0:T(4,128)S(1)} collective-permute-done((f32[4,512]{1,0:T(4,128)S(1)}, f32[4,512]{1,0:T(4,128)S(1)}, u32[]{:S(2)}, u32[]{:S(2)}) %collective-permute-start.10) | collective-permute-done | bytes 8224 | tf_op jit(solution)/shard_map/ppermute | solution.py:19
  72.3 3.6 %far_weights.1 = (bf16[384,512]{1,0:T(8,128)(2,1)S(1)}, bf16[384,512]{1,0:T(8,128)(2,1)S(1)}, bf16[384,1536]{1,0:T(8,128)(2,1)S(1)}, bf16[1536,384]{1,0:T(8,128)(2,1)S(1)}) custom-call(f32[4,384,128]{2,1,0:T(8,128)S(1)} %broadcast_in_dim.30.row_inv, f32[4,1,384]{2,1,0:T(1,128)S(1)} %fusion.3.col_inv, bf16[7,384,384]{2,1,0:T(8,128)(2,1)} %get-tuple-element.50.far, ...), custom_call_target="tpu_custom_call" | custom-call | flops 1207959552 | bytes 12582912 | tf_op jit(solution)/shard_map/far_weights/pallas_call | solution.py:309
  78.2 7.1 %near_weights.1 = (bf16[384,512]{1,0:T(8,128)(2,1)}, bf16[384,512]{1,0:T(8,128)(2,1)}, bf16[384,512]{1,0:T(8,128)(2,1)}, bf16[384,512]{1,0:T(8,128)(2,1)}, bf16[1152,1152]{1,0:T(8,128)(2,1)}) custom-call(s32[384,1]{1,0:T(8,128)S(1)} %copy-done.11, f32[4,384,128]{2,1,0:T(8,128)S(1)} %broadcast_in_dim.30.row_inv, f32[4,1,384]{2,1,0:T(1,128)S(1)} %fusion.3.col_inv, ...), custom_call_target="tpu_custom_call" | custom-call | flops 3623878656 | bytes 12582912 | tf_op jit(solution)/shard_map/near_weights/pallas_call | solution.py:309
  96.0 4.0 %own_weights.1 = (f32[384,512]{1,0:T(8,128)S(1)}, f32[384,512]{1,0:T(8,128)S(1)}) custom-call(bf16[1152,1152]{1,0:T(8,128)(2,1)} %get-tuple-element.63.refs_0_, bf16[384,1536]{1,0:T(8,128)(2,1)S(1)} %get-tuple-element.55.wide.refs_1_, bf16[1536,384]{1,0:T(8,128)(2,1)S(1)} %copy-done.2, bf16[1152,512]{1,0:T(8,128)(2,1)} %get-tuple-element.51.rows_near.refs_0_.refs_3_, ...), custom_call_target="tpu_custom_call" | custom-call | flops 1207959552 | bytes 12582912 | tf_op jit(solution)/shard_map/own_weights/pallas_call | solution.py:309
  100.0 3.5 %collective-permute-done.17.refs_3_ = bf16[384,512]{1,0:T(8,128)(2,1)} collective-permute-done((bf16[384,512]{1,0:T(8,128)(2,1)}, bf16[384,512]{1,0:T(8,128)(2,1)}, u32[]{:S(2)}, u32[]{:S(2)}) %collective-permute-start.17) | collective-permute-done | bytes 393248 | tf_op jit(solution)/shard_map/ppermute | solution.py:19
  103.5 2.6 %row_gradients.1 = (bf16[384,1024]{1,0:T(8,128)(2,1)S(1)}, bf16[400,512]{1,0:T(8,128)(2,1)S(1)}, bf16[384,512]{1,0:T(8,128)(2,1)S(1)}) custom-call(f32[1]{0:T(128)S(6)} %copy.21.refs_1_.scale, s32[1]{0:T(128)} %bitcast.15.core, f32[1]{0:T(128)} %bitcast.16.ring_loss, f32[384,512]{1,0:T(8,128)S(1)} %get-tuple-element.66.by_row, ...), custom_call_target="tpu_custom_call" | custom-call | flops 150994944 | bytes 12582912 | tf_op jit(solution)/shard_map/row_gradients/pallas_call | solution.py:309
  111.4 8.6 %hidden_grad.1 = bf16[384,3584]{1,0:T(8,128)(2,1)} custom-call(bf16[384,1024]{1,0:T(8,128)(2,1)S(1)} %get-tuple-element.74.rows, bf16[3584,1024]{1,0:T(8,128)(2,1)} %weights.1), custom_call_target="tpu_custom_call" | custom-call | flops 2818572288 | bytes 11534336 | tf_op jit(solution)/shard_map/hidden_grad/pallas_call | solution.py:235
  120.0 9.3 %collective-permute-done.22.refs_1_.back = bf16[784,512]{1,0:T(8,128)(2,1)S(1)} collective-permute-done((bf16[784,512]{1,0:T(8,128)(2,1)S(1)}, bf16[784,512]{1,0:T(8,128)(2,1)S(1)}, u32[]{:S(2)}, u32[]{:S(2)}) %collective-permute-start.22) | collective-permute-done | bytes 802848 | tf_op jit(solution)/shard_map/ppermute | solution.py:19
  129.9 3.0 %collective-permute-start.25 = (bf16[384,512]{1,0:T(8,128)(2,1)S(1)}, bf16[384,512]{1,0:T(8,128)(2,1)S(1)}, u32[]{:S(2)}, u32[]{:S(2)}) collective-permute-start(bf16[384,512]{1,0:T(8,128)(2,1)S(1)} %slice.139), channel_id=1, source_target_pairs={{0,96},{32,0},{64,32},{96,64},{1,97},{33,1},{65,33},{97,65},{2,98}... | collective-permute-start | bytes 1179656 | tf_op jit(solution)/shard_map/ppermute | solution.py:19
  132.9 5.5 %near_rows.1.first = f32[896,512]{1,0:T(8,128)S(1)} custom-call(s32[3]{0:T(128)S(1)} %pad_add_fusion.places, bf16[4,384,896]{2,1,0:T(8,128)(2,1)} %all-to-all-done.hidden_own, bf16[4,384,896]{2,1,0:T(8,128)(2,1)} %collective-permute-done.18.hidden_other, bf16[784,512]{1,0:T(8,128)(2,1)S(1)} %constant_dynamic-update-slice_fusion.refs_0_.pair, ...), custom_call_target="tpu_custom_call" | custom-call | flops 21139292160 | bytes 8388608 | tf_op jit(solution)/shard_map/near_rows/pallas_call | solution.py:289
  138.4 2.1 %collective-permute-done.25.other = bf16[384,512]{1,0:T(8,128)(2,1)S(1)} collective-permute-done((bf16[384,512]{1,0:T(8,128)(2,1)S(1)}, bf16[384,512]{1,0:T(8,128)(2,1)S(1)}, u32[]{:S(2)}, u32[]{:S(2)}) %collective-permute-start.25) | collective-permute-done | bytes 393248 | tf_op jit(solution)/shard_map/ppermute | solution.py:19
  141.6 2.5 %last_rows.1 = bf16[32,32,512]{2,1,0:T(8,128)(2,1)S(1)} custom-call(s32[1]{0:T(128)} %bitcast.places, bf16[4,384,896]{2,1,0:T(8,128)(2,1)} %all-to-all-done.hidden_own, bf16[4,384,896]{2,1,0:T(8,128)(2,1)} %collective-permute-done.18.hidden_other, bf16[400,512]{1,0:T(8,128)(2,1)S(1)} %collective-permute-done.24.own, ...), custom_call_target="tpu_custom_call" | custom-call | flops 704643072 | bytes 8388608 | tf_op jit(solution)/shard_map/last_rows/pallas_call | solution.py:289
  144.0 20.8 %all_to_all.10 = bf16[32,32,512]{2,1,0:T(8,128)(2,1)S(1)} all-to-all(bf16[32,32,512]{2,1,0:T(8,128)(2,1)S(1)} %last_rows.1), channel_id=1, replica_groups=mesh['y'=4,'core'=2,'z'=4,'x'=4] {'core','z','x'}, dimensions={0} | all-to-all | bytes 2097152 | tf_op jit(solution)/shard_map/all_to_all | solution.py:423
  (122 shorter events, 44.0 us)
Async XLA Ops:
  8.4 20.4 %collective-permute-start = (bf16[384,1024]{1,0:T(8,128)(2,1)S(1)}, bf16[384,1024]{1,0:T(8,128)(2,1)S(1)}, u32[]{:S(2)}, u32[]{:S(2)}) collective-permute-start(bf16[384,1024]{1,0:T(8,128)(2,1)S(1)} %get-tuple-element.79.refs_3_.refs_6_.refs_8_), channel_id=1, source_target_pairs={{0,1},{1,2},{2,3},{3,0},{4,5},{5,6},{6,7},{7,4},{8,9},{9,10},{10,1... | collective-permute-start | bytes 2359304 | tf_op jit(solution)/shard_map/ppermute | solution.py:19
  10.0 20.1 %collective-permute-start.1 = (bf16[384,1024]{1,0:T(8,128)(2,1)S(1)}, bf16[384,1024]{1,0:T(8,128)(2,1)S(1)}, u32[]{:S(2)}, u32[]{:S(2)}) collective-permute-start(bf16[384,1024]{1,0:T(8,128)(2,1)S(1)} %get-tuple-element.79.refs_3_.refs_6_.refs_8_), channel_id=1, source_target_pairs={{0,3},{1,0},{2,1},{3,2},{4,7},{5,4},{6,5},{7,6},{8,11},{9,8},{10,9... | collective-permute-start | bytes 2359304 | tf_op jit(solution)/shard_map/ppermute | solution.py:19
  11.6 22.0 %collective-permute-start.2 = (bf16[384,1024]{1,0:T(8,128)(2,1)S(1)}, bf16[384,1024]{1,0:T(8,128)(2,1)S(1)}, u32[]{:S(2)}, u32[]{:S(2)}) collective-permute-start(bf16[384,1024]{1,0:T(8,128)(2,1)S(1)} %get-tuple-element.79.refs_3_.refs_6_.refs_8_), channel_id=1, source_target_pairs={{0,4},{4,8},{8,12},{12,0},{1,5},{5,9},{9,13},{13,1},{2,6},{6,10},{... | collective-permute-start | bytes 2359304 | tf_op jit(solution)/shard_map/ppermute | solution.py:19
  13.6 23.0 %collective-permute-start.3 = (bf16[384,1024]{1,0:T(8,128)(2,1)S(1)}, bf16[384,1024]{1,0:T(8,128)(2,1)}, u32[]{:S(2)}, u32[]{:S(2)}) collective-permute-start(bf16[384,1024]{1,0:T(8,128)(2,1)S(1)} %get-tuple-element.79.refs_3_.refs_6_.refs_8_), channel_id=1, source_target_pairs={{0,12},{4,0},{8,4},{12,8},{1,13},{5,1},{9,5},{13,9},{2,14},{6,2},{... | collective-permute-start | bytes 2359304 | tf_op jit(solution)/shard_map/ppermute | solution.py:19
  17.7 54.1 %all-to-all-start = ((bf16[4,384,896]{2,1,0:T(8,128)(2,1)}), bf16[4,384,896]{2,1,0:T(8,128)(2,1)}, u32[]{:S(2)}, u32[]{:S(2)}) async-start(bf16[4,384,896]{2,1,0:T(8,128)(2,1)} %pad_maximum_fusion), calls=%async_computation | async-start | bytes 5505024 | tf_op jit(solution)/shard_map/all_to_all | solution.py:347
  29.5 21.9 %collective-permute-start.4 = (bf16[192,1024]{1,0:T(8,128)(2,1)}, bf16[192,1024]{1,0:T(8,128)(2,1)}, u32[]{:S(2)}, u32[]{:S(2)}) collective-permute-start(bf16[192,1024]{1,0:T(8,128)(2,1)} %slice.120), channel_id=1, source_target_pairs={{0,1},{1,2},{2,3},{3,0},{4,5},{5,6},{6,7},{7,4},{8,9},{9,10},{10,1... | collective-permute-start | bytes 1179656 | tf_op jit(solution)/shard_map/ppermute | solution.py:19
  30.9 20.6 %collective-permute-start.5 = (bf16[192,1024]{1,0:T(8,128)(2,1)}, bf16[192,1024]{1,0:T(8,128)(2,1)}, u32[]{:S(2)}, u32[]{:S(2)}) collective-permute-start(bf16[192,1024]{1,0:T(8,128)(2,1)} %slice.121), channel_id=1, source_target_pairs={{0,3},{1,0},{2,1},{3,2},{4,7},{5,4},{6,5},{7,6},{8,11},{9,8},{10,9... | collective-permute-start | bytes 1179656 | tf_op jit(solution)/shard_map/ppermute | solution.py:19
  34.5 17.0 %collective-permute-start.6 = (bf16[192,1024]{1,0:T(8,128)(2,1)}, bf16[192,1024]{1,0:T(8,128)(2,1)}, u32[]{:S(2)}, u32[]{:S(2)}) collective-permute-start(bf16[192,1024]{1,0:T(8,128)(2,1)} %slice.122), channel_id=1, source_target_pairs={{0,4},{4,8},{8,12},{12,0},{1,5},{5,9},{9,13},{13,1},{2,6},{6,10},{... | collective-permute-start | bytes 1179656 | tf_op jit(solution)/shard_map/ppermute | solution.py:19
  38.4 13.2 %collective-permute-start.7 = (bf16[192,1024]{1,0:T(8,128)(2,1)}, bf16[192,1024]{1,0:T(8,128)(2,1)}, u32[]{:S(2)}, u32[]{:S(2)}) collective-permute-start(bf16[192,1024]{1,0:T(8,128)(2,1)} %slice.123), channel_id=1, source_target_pairs={{0,12},{4,0},{8,4},{12,8},{1,13},{5,1},{9,5},{13,9},{2,14},{6,2},{... | collective-permute-start | bytes 1179656 | tf_op jit(solution)/shard_map/ppermute | solution.py:19
  60.0 7.7 %collective-permute-start.12 = (f32[4,384]{1,0:T(4,128)S(1)}, f32[4,384]{1,0:T(4,128)S(1)}, u32[]{:S(2)}, u32[]{:S(2)}) collective-permute-start(f32[4,384]{1,0:T(4,128)S(1)} %add_reduce_fusion.1), channel_id=1, source_target_pairs={{0,8},{4,12},{8,0},{12,4},{1,9},{5,13},{9,1},{13,5},{2,10},{6,14},... | collective-permute-start | bytes 18440 | tf_op jit(solution)/shard_map/ppermute | solution.py:19
  62.9 4.8 %collective-permute-start.13 = (f32[4,384]{1,0:T(4,128)S(1)}, f32[4,384]{1,0:T(4,128)S(1)}, u32[]{:S(2)}, u32[]{:S(2)}) collective-permute-start(f32[4,384]{1,0:T(4,128)S(1)} %add_reduce_fusion.1), channel_id=1, source_target_pairs={{0,4},{4,8},{8,12},{12,0},{1,5},{5,9},{9,13},{13,1},{2,6},{6,10},{... | collective-permute-start | bytes 18440 | tf_op jit(solution)/shard_map/ppermute | solution.py:19
  64.6 6.7 %collective-permute-start.9 = (f32[4,512]{1,0:T(4,128)S(1)}, f32[4,512]{1,0:T(4,128)S(1)}, u32[]{:S(2)}, u32[]{:S(2)}) collective-permute-start(f32[4,512]{1,0:T(4,128)S(1)} %pad_maximum_fusion.2), channel_id=1, source_target_pairs={{0,2},{1,3},{2,0},{3,1},{4,6},{5,7},{6,4},{7,5},{8,10},{9,11},{10,... | collective-permute-start | bytes 24584 | tf_op jit(solution)/shard_map/ppermute | solution.py:19
  66.3 4.9 %collective-permute-start.10 = (f32[4,512]{1,0:T(4,128)S(1)}, f32[4,512]{1,0:T(4,128)S(1)}, u32[]{:S(2)}, u32[]{:S(2)}) collective-permute-start(f32[4,512]{1,0:T(4,128)S(1)} %pad_maximum_fusion.2), channel_id=1, source_target_pairs={{0,1},{1,2},{2,3},{3,0},{4,5},{5,6},{6,7},{7,4},{8,9},{9,10},{10,1... | collective-permute-start | bytes 24584 | tf_op jit(solution)/shard_map/ppermute | solution.py:19
  72.1 31.4 %collective-permute-start.18 = (bf16[4,384,896]{2,1,0:T(8,128)(2,1)}, bf16[4,384,896]{2,1,0:T(8,128)(2,1)}, u32[]{:S(2)}, u32[]{:S(2)}) collective-permute-start(bf16[4,384,896]{2,1,0:T(8,128)(2,1)} %all-to-all-done.hidden_own), channel_id=1, source_target_pairs={{0,16},{16,0},{1,17},{17,1},{2,18},{18,2},{3,19},{19,3},{4,20},{20... | collective-permute-start | bytes 8257544 | tf_op jit(solution)/shard_map/ppermute | solution.py:23
  75.8 13.1 %collective-permute-start.19 = (bf16[384,512]{1,0:T(8,128)(2,1)S(1)}, bf16[384,512]{1,0:T(8,128)(2,1)S(1)}, u32[]{:S(2)}, u32[]{:S(2)}) collective-permute-start(bf16[384,512]{1,0:T(8,128)(2,1)S(1)} %get-tuple-element.64), channel_id=1, source_target_pairs={{0,2},{1,3},{2,0},{3,1},{4,6},{5,7},{6,4},{7,5},{8,10},{9,11},{10,... | collective-permute-start | bytes 1179656 | tf_op jit(solution)/shard_map/ppermute | solution.py:19
  76.5 14.3 %collective-permute-start.20 = (bf16[384,512]{1,0:T(8,128)(2,1)S(1)}, bf16[384,512]{1,0:T(8,128)(2,1)S(1)}, u32[]{:S(2)}, u32[]{:S(2)}) collective-permute-start(bf16[384,512]{1,0:T(8,128)(2,1)S(1)} %get-tuple-element.65), channel_id=1, source_target_pairs={{0,8},{4,12},{8,0},{12,4},{1,9},{5,13},{9,1},{13,5},{2,10},{6,14},... | collective-permute-start | bytes 1179656 | tf_op jit(solution)/shard_map/ppermute | solution.py:19
  85.3 14.7 %collective-permute-start.14 = (bf16[384,512]{1,0:T(8,128)(2,1)}, bf16[384,512]{1,0:T(8,128)(2,1)}, u32[]{:S(2)}, u32[]{:S(2)}) collective-permute-start(bf16[384,512]{1,0:T(8,128)(2,1)} %get-tuple-element.57), channel_id=1, source_target_pairs={{0,3},{1,0},{2,1},{3,2},{4,7},{5,4},{6,5},{7,6},{8,11},{9,8},{10,9... | collective-permute-start | bytes 1179656 | tf_op jit(solution)/shard_map/ppermute | solution.py:19
  87.0 13.0 %collective-permute-start.15 = (bf16[384,512]{1,0:T(8,128)(2,1)}, bf16[384,512]{1,0:T(8,128)(2,1)}, u32[]{:S(2)}, u32[]{:S(2)}) collective-permute-start(bf16[384,512]{1,0:T(8,128)(2,1)} %get-tuple-element.58), channel_id=1, source_target_pairs={{0,1},{1,2},{2,3},{3,0},{4,5},{5,6},{6,7},{7,4},{8,9},{9,10},{10,1... | collective-permute-start | bytes 1179656 | tf_op jit(solution)/shard_map/ppermute | solution.py:19
  88.9 11.1 %collective-permute-start.16 = (bf16[384,512]{1,0:T(8,128)(2,1)}, bf16[384,512]{1,0:T(8,128)(2,1)}, u32[]{:S(2)}, u32[]{:S(2)}) collective-permute-start(bf16[384,512]{1,0:T(8,128)(2,1)} %get-tuple-element.59), channel_id=1, source_target_pairs={{0,12},{4,0},{8,4},{12,8},{1,13},{5,1},{9,5},{13,9},{2,14},{6,2},{... | collective-permute-start | bytes 1179656 | tf_op jit(solution)/shard_map/ppermute | solution.py:19
  91.6 12.0 %collective-permute-start.17 = (bf16[384,512]{1,0:T(8,128)(2,1)}, bf16[384,512]{1,0:T(8,128)(2,1)}, u32[]{:S(2)}, u32[]{:S(2)}) collective-permute-start(bf16[384,512]{1,0:T(8,128)(2,1)} %get-tuple-element.60), channel_id=1, source_target_pairs={{0,4},{4,8},{8,12},{12,0},{1,5},{5,9},{9,13},{13,1},{2,6},{6,10},{... | collective-permute-start | bytes 1179656 | tf_op jit(solution)/shard_map/ppermute | solution.py:19
  108.0 21.3 %collective-permute-start.22 = (bf16[784,512]{1,0:T(8,128)(2,1)S(1)}, bf16[784,512]{1,0:T(8,128)(2,1)S(1)}, u32[]{:S(2)}, u32[]{:S(2)}) collective-permute-start(bf16[784,512]{1,0:T(8,128)(2,1)S(1)} %constant_dynamic-update-slice_fusion.refs_0_.pair), channel_id=1, source_target_pairs={{0,32},{32,64},{64,96},{96,0},{1,33},{33,65},{65,97},{97,1},{2,34}... | collective-permute-start | bytes 2408456 | tf_op jit(solution)/shard_map/ppermute | solution.py:19
  109.6 20.3 %collective-permute-start.23 = (bf16[784,512]{1,0:T(8,128)(2,1)S(1)}, bf16[784,512]{1,0:T(8,128)(2,1)S(1)}, u32[]{:S(2)}, u32[]{:S(2)}) collective-permute-start(bf16[784,512]{1,0:T(8,128)(2,1)S(1)} %constant_dynamic-update-slice_fusion.refs_0_.pair), channel_id=1, source_target_pairs={{0,96},{32,0},{64,32},{96,64},{1,97},{33,1},{65,33},{97,65},{2,98}... | collective-permute-start | bytes 2408456 | tf_op jit(solution)/shard_map/ppermute | solution.py:19
  129.3 12.3 %collective-permute-start.24 = (bf16[400,512]{1,0:T(8,128)(2,1)S(1)}, bf16[400,512]{1,0:T(8,128)(2,1)S(1)}, u32[]{:S(2)}, u32[]{:S(2)}) collective-permute-start(bf16[400,512]{1,0:T(8,128)(2,1)S(1)} %slice.138), channel_id=1, source_target_pairs={{0,32},{32,64},{64,96},{96,0},{1,33},{33,65},{65,97},{97,1},{2,34}... | collective-permute-start | bytes 1228808 | tf_op jit(solution)/shard_map/ppermute | solution.py:19
  129.9 10.6 %collective-permute-start.25 = (bf16[384,512]{1,0:T(8,128)(2,1)S(1)}, bf16[384,512]{1,0:T(8,128)(2,1)S(1)}, u32[]{:S(2)}, u32[]{:S(2)}) collective-permute-start(bf16[384,512]{1,0:T(8,128)(2,1)S(1)} %slice.139), channel_id=1, source_target_pairs={{0,96},{32,0},{64,32},{96,64},{1,97},{33,1},{65,33},{97,65},{2,98}... | collective-permute-start | bytes 1179656 | tf_op jit(solution)/shard_map/ppermute | solution.py:19
  (20 other events, 106.7 us)

commit v2 on v1

--- a/solution.py
+++ b/solution.py
@@ -16,7 +16,10 @@
 
 
 def send(array, axis, step):
-    return lax.ppermute(array, axis, [(i, (i + step) % 4) for i in range(4)])
+    pairs = [(core, i, (i + (1 - 2 * core) * step) % 4) for core in range(2) for i in range(4)]
+    if axis == "y":
+        return lax.ppermute(array, ("y", "core"), [(2 * i + core, 2 * j + core) for core, i, j in pairs])
+    return lax.ppermute(array, ("core", axis), [(4 * core + i, 4 * core + j) for core, i, j in pairs])
 
 
 def swap(array):
@@ -24,12 +27,9 @@
 
 
 def ring_gather(block, axis):
-    half = block.shape[0] // 2
     back = send(block, axis, 1)
     ahead = send(block, axis, -1)
-    far_top = send(back[:half], axis, 1)
-    far_bottom = send(ahead[half:], axis, -1)
-    return (back,), (far_top, far_bottom), (ahead,)
+    return (back,), (send(back, axis, 1),), (ahead,)
 
 
 def ring_total(parts, axis):
@@ -107,7 +107,7 @@
     ]
     out_shape += [jax.ShapeDtypeStruct(((1 if final else 3) * rows, width // 2), jnp.bfloat16)] * 2
     out_shape += [jax.ShapeDtypeStruct((8 if final else rows, 128), jnp.float32)]
-    scratch = [pltpu.VMEM((rows, width), jnp.bfloat16)] * 2 if final else []
+    scratch = []
     pieces = [len(row_pieces[d]) for d in names]
     return pl.pallas_call(
         functools.partial(score_kernel, tiles, names, pieces, final),
@@ -250,31 +250,31 @@
 
 
 def gather_kernel(places, hidden_own, hidden_other, *refs):
-    pairs, out = refs[:3], refs[3]
+    own, other, out = refs[:3], refs[3:6], refs[6]
     rows = hidden_own.shape[1]
     step = pl.program_id(0)
     for k in range(3):
         @pl.when(step == k)
         def _():
-            made = product_over_rows(hidden_own[0], pairs[k][:rows])
-            made = made + product_over_rows(hidden_other[0], pairs[k][rows + 16 :])
+            made = product_over_rows(hidden_own[0], own[k][:rows])
+            made = made + product_over_rows(hidden_other[0], other[k][...])
             if k == 0:
                 out[...] = made
             else:
                 out[...] += made
 
 
-def last_kernel(places, hidden_own, hidden_other, own, other, pair, back, ahead, first, out, total):
-    rows = other.shape[0]
+def last_kernel(places, hidden_own, hidden_other, far, other_far, kept, back, ahead, first, out, total):
+    rows = hidden_own.shape[1]
     total[...] = (
         first[...]
-        + product_over_rows(hidden_own[0], own[:rows])
-        + product_over_rows(hidden_other[0], other[...])
-    )
-    loss = jnp.zeros((1, own.shape[1]), jnp.float32)
-    for source in (own, pair, back, ahead):
+        + product_over_rows(hidden_own[0], far[:rows])
+        + product_over_rows(hidden_other[0], other_far[...])
+    )
+    loss = jnp.zeros((1, far.shape[1]), jnp.float32)
+    for source in (far, kept, back, ahead):
         loss = loss + jnp.sum(source[rows : rows + 16].astype(jnp.float32), axis=0, keepdims=True)
-    spare = split_value(jnp.broadcast_to(loss, (16, own.shape[1])))[:4]
+    spare = split_value(jnp.broadcast_to(loss, (16, far.shape[1])))[:4]
     count, padded = out.shape[:2]
     size = padded - 4
     for k in range(count):
@@ -328,8 +328,9 @@
 
     offsets = (partners[0] % 16) ^ mine
     back = jnp.arange(4)
-    row_ids = iz * 4 + (ix - back) % 4
-    col_ids = ((iz - back) % 4) * 4 + ix
+    way = 1 - 2 * ic
+    row_ids = iz * 4 + (ix - way * back) % 4
+    col_ids = ((iz - way * back) % 4) * 4 + ix
     apart = (row_ids[:, None] ^ col_ids[None, :]).reshape(16)
     active = (jnp.any(apart[:, None] == offsets[None, :], axis=1) | (apart == 0)).astype(jnp.int32)
     pos = (positives % rows)[:, None]
@@ -402,21 +403,21 @@
         ),
         scalars=3,
     )
-    pair = jnp.concatenate([kept, swap(other)], axis=0)
+    own_back, own_ahead = send(kept, "y", 1), send(kept, "y", -1)
+    other = swap(other)
+    other_back, other_ahead = send(other, "y", 1), send(other, "y", -1)
     grad_hidden = hidden_grad(grad_projected, projection)
-    pair_back, pair_ahead = send(pair, "y", 1), send(pair, "y", -1)
-    own_far = send(pair_back[: rows + 16], "y", 1)
-    other_far = send(pair_ahead[rows + 16 :], "y", -1)
+    own_far, other_far = send(own_back, "y", 1), send(other_back, "y", 1)
     step = 2 * rows * fourth * half
     first = call_by_place(
-        gather_kernel, "near_rows", 60 * step, jnp.stack([iy, (iy + 3) % 4, (iy + 1) % 4]),
-        own_hidden, other_hidden, (pair, pair_back, pair_ahead),
+        gather_kernel, "near_rows", 60 * step, jnp.stack([iy, (iy - way) % 4, (iy + way) % 4]),
+        own_hidden, other_hidden, (kept, own_back, own_ahead, other, other_back, other_ahead),
         jax.ShapeDtypeStruct((fourth, half), jnp.float32),
     )
     first, own_far, other_far, grad_hidden = lax.optimization_barrier((first, own_far, other_far, grad_hidden))
     part = call_by_place(
         last_kernel, "last_rows", 2 * step, ((iy + 2) % 4)[None], own_hidden, other_hidden,
-        (own_far, other_far, pair, pair_back, pair_ahead, first),
+        (own_far, other_far, kept, own_back, own_ahead, first),
         jax.ShapeDtypeStruct((32, fourth // 32 + 4, half), jnp.bfloat16),
         scratch=[pltpu.VMEM((fourth, half), jnp.float32)],
     )

time: 169 us -> 162 us (0.959)
  waiting for transfers between devices: 29.1 us -> 22 us
  blocking collectives: 20.8 us -> 22.6 us
    ppermute x24, waiting for transfers between devices: 27.4 us -> 22 us  [the longest x18 13.9 us: send(): lax.ppermute(array, ('core', axis), [(4 * core + i, 4 * core + j) for cor...]
    slice x6 -> x0, local copies, waits for them, and re-layouts: 4.28 us -> none  [the longest x2 2.61 us: ring_gather(): far_bottom = send(ahead[half:], axis, -1)]
    unnamed x35 -> x34, local copies, waits for them, and re-layouts: 6.26 us -> 9.35 us
    all_to_all x1, blocking collectives: 20.8 us -> 22.6 us  [per_device(): arrived = lax.all_to_all(part, ('core', 'z', 'x'), 0, 0).astype(jnp.float32)]
  transfers between devices with their start and end apart: 27 -> 27, of which waited for: 10 -> 10; matrix products, arithmetic and copies ran while one was open for 6% -> 3% of each run, Pallas kernels for 26% -> 27%
where the time goes in v2:
time: 162 us
  Pallas kernels  48.1 us (30%)
  starting transfers between devices  39.8 us (25%)
  blocking collectives  22.6 us (14%)
  waiting for transfers between devices  22 us (14%)
  local copies, waits for them, and re-layouts  10.2 us (6%)
  other arithmetic  7.88 us (5%)
  matrix products  6.26 us (4%)
  between operations  4.72 us (3%)
    ppermute x18, starting transfers between devices, send(): lax.ppermute(array, ('core', axis), [(4 * core + i, 4 * core + j) for cor...  26.6 us
    all_to_all x1, blocking collectives, per_device(): arrived = lax.all_to_all(part, ('core', 'z', 'x'), 0, 0).astype(jnp.float32)  22.6 us
    pallas_call x4, Pallas kernels, call(): pl.pallas_call(kernel, out_shape=out_shape, in_specs=[smem] * scalars + [...  17.3 us
    pallas_call x2, Pallas kernels, score_tiles(): pl.pallas_call(functools.partial(score_kernel, tiles, names, pieces, fina...  14.2 us
    ppermute x18, waiting for transfers between devices, send(): lax.ppermute(array, ('core', axis), [(4 * core + i, 4 * core + j) for cor...  13.9 us
    unnamed x34, local copies, waits for them, and re-layouts  9.35 us
    pallas_call x1, Pallas kernels, hidden_grad(): pl.pallas_call(hidden_kernel, grid=(steps,), out_shape=jax.ShapeDtypeStru...  8.58 us
    ppermute x6, starting transfers between devices, send(): lax.ppermute(array, ('y', 'core'), [(2 * i + core, 2 * j + core) for core...  8.29 us
  transfers between devices with their start and end apart: 27, of which 10 were waited for; matrix products, arithmetic and copies ran while one was open for 3% of the time, Pallas kernels for 27%

profile of v2, /device:TPU:0, one launch (start us, length us, event | category | flops | bytes accessed | tf_op | source)
XLA Modules:
  0.0 161.6 jit_solution(10161379981410370462)
XLA Ops:
  0.6 6.3 %multiply_reduce_fusion = (f32[384]{0:T(512)S(1)}, f32[384,1024]{1,0:T(8,128)S(1)}) fusion(bf16[384,3584]{1,0:T(8,128)(2,1)} %param.5, bf16[3584,1024]{1,0:T(8,128)(2,1)} %weights.1), kind=kOutput, calls=%fused_computation.2 | convolution fusion | flops 2819358208 | bytes 11666944 | tf_op jit(solution)/shard_map/dot_general | solution.py:338
  13.6 2.1 %collective-permute-start.3 = (bf16[384,1024]{1,0:T(8,128)(2,1)S(1)}, bf16[384,1024]{1,0:T(8,128)(2,1)S(1)}, u32[]{:S(2)}, u32[]{:S(2)}) collective-permute-start(bf16[384,1024]{1,0:T(8,128)(2,1)S(1)} %get-tuple-element.79.refs_3_.refs_6_.refs_7_), channel_id=1, source_target_pairs={{0,12},{4,0},{8,4},{12,8},{16,20},{20,24},{24,28},{28,16},{1,13},{... | collective-permute-start | bytes 2359304 | tf_op jit(solution)/shard_map/ppermute | solution.py:22
  17.7 4.7 %all-to-all-start = ((bf16[4,384,896]{2,1,0:T(8,128)(2,1)}), bf16[4,384,896]{2,1,0:T(8,128)(2,1)}, u32[]{:S(2)}, u32[]{:S(2)}) async-start(bf16[4,384,896]{2,1,0:T(8,128)(2,1)} %pad_maximum_fusion), calls=%async_computation | async-start | bytes 5505024 | tf_op jit(solution)/shard_map/all_to_all | solution.py:348
  22.6 2.2 %collective-permute-done.refs_4_ = bf16[384,1024]{1,0:T(8,128)(2,1)S(1)} collective-permute-done((bf16[384,1024]{1,0:T(8,128)(2,1)S(1)}, bf16[384,1024]{1,0:T(8,128)(2,1)S(1)}, u32[]{:S(2)}, u32[]{:S(2)}) %collective-permute-start) | collective-permute-done | bytes 786464 | tf_op jit(solution)/shard_map/ppermute | solution.py:22
  26.4 3.2 %collective-permute-done.2.refs_7_.refs_8_ = bf16[384,1024]{1,0:T(8,128)(2,1)} collective-permute-done((bf16[384,1024]{1,0:T(8,128)(2,1)S(1)}, bf16[384,1024]{1,0:T(8,128)(2,1)}, u32[]{:S(2)}, u32[]{:S(2)}) %collective-permute-start.2) | collective-permute-done | bytes 786464 | tf_op jit(solution)/shard_map/ppermute | solution.py:22
  29.6 2.5 %collective-permute-start.5 = (bf16[384,1024]{1,0:T(8,128)(2,1)}, bf16[384,1024]{1,0:T(8,128)(2,1)}, u32[]{:S(2)}, u32[]{:S(2)}) collective-permute-start(bf16[384,1024]{1,0:T(8,128)(2,1)} %collective-permute-done.2.refs_7_.refs_8_), channel_id=1, source_target_pairs={{0,4},{4,8},{8,12},{12,0},{16,28},{20,16},{24,20},{28,24},{1,5},{5... | collective-permute-start | bytes 2359304 | tf_op jit(solution)/shard_map/ppermute | solution.py:22
  37.3 7.7 %scores.2 = (bf16[9,384,384]{2,1,0:T(8,128)(2,1)}, f32[4,384,128]{2,1,0:T(8,128)S(1)}, f32[4,8,384]{2,1,0:T(8,128)S(1)}, bf16[1152,512]{1,0:T(8,128)(2,1)}, bf16...) custom-call(s32[16]{0:T(128)S(1)} %or_convert_fusion.refs_0_, f32[1]{0:T(128)S(6)} %copy.20.refs_1_.scale, ...), custom_call_target="tpu_custom_call" | custom-call | flops 2717908992 | bytes 16777216 | tf_op jit(solution)/shard_map/scores/pallas_call | solution.py:112
  48.5 6.6 %scores.3 = (bf16[7,384,384]{2,1,0:T(8,128)(2,1)}, f32[4,384,128]{2,1,0:T(8,128)S(1)}, f32[4,8,384]{2,1,0:T(8,128)S(1)}, bf16[384,512]{1,0:T(8,128)(2,1)S(1)}, b...) custom-call(s32[16]{0:T(128)S(1)} %or_convert_fusion.refs_0_, f32[1]{0:T(128)S(6)} %copy.20.refs_1_.scale, ...), custom_call_target="tpu_custom_call" | custom-call | flops 2113929216 | bytes 16777216 | tf_op jit(solution)/shard_map/scores/pallas_call | solution.py:112
  55.1 3.9 %collective-permute-start.10 = (f32[4,384]{1,0:T(4,128)S(1)}, f32[4,384]{1,0:T(4,128)S(1)}, u32[]{:S(2)}, u32[]{:S(2)}) collective-permute-start(f32[4,384]{1,0:T(4,128)S(1)} %add_reduce_fusion.1), channel_id=1, source_target_pairs={{0,8},{4,12},{8,0},{12,4},{16,24},{20,28},{24,16},{28,20},{1,9},{5... | collective-permute-start | bytes 18440 | tf_op jit(solution)/shard_map/ppermute | solution.py:22
  61.4 2.2 %collective-permute-start.7 = (f32[4,512]{1,0:T(4,128)S(1)}, f32[4,512]{1,0:T(4,128)S(1)}, u32[]{:S(2)}, u32[]{:S(2)}) collective-permute-start(f32[4,512]{1,0:T(4,128)S(1)} %pad_maximum_fusion.2), channel_id=1, source_target_pairs={{0,2},{1,3},{2,0},{3,1},{16,18},{17,19},{18,16},{19,17},{4,6},{5,7... | collective-permute-start | bytes 24584 | tf_op jit(solution)/shard_map/ppermute | solution.py:22
  67.3 2.3 %collective-permute-done.8 = f32[4,512]{1,0:T(4,128)S(1)} collective-permute-done((f32[4,512]{1,0:T(4,128)S(1)}, f32[4,512]{1,0:T(4,128)S(1)}, u32[]{:S(2)}, u32[]{:S(2)}) %collective-permute-start.8) | collective-permute-done | bytes 8224 | tf_op jit(solution)/shard_map/ppermute | solution.py:22
  70.7 3.6 %far_weights.1 = (bf16[384,512]{1,0:T(8,128)(2,1)S(1)}, bf16[384,512]{1,0:T(8,128)(2,1)S(1)}, bf16[384,1536]{1,0:T(8,128)(2,1)S(1)}, bf16[1536,384]{1,0:T(8,128)(2,1)S(1)}) custom-call(f32[4,384,128]{2,1,0:T(8,128)S(1)} %broadcast_in_dim.30.row_inv, f32[4,1,384]{2,1,0:T(1,128)S(1)} %fusion.3.col_inv, bf16[7,384,384]{2,1,0:T(8,128)(2,1)} %get-tuple-element.50.far, ...), custom_call_target="tpu_custom_call" | custom-call | flops 1207959552 | bytes 12582912 | tf_op jit(solution)/shard_map/far_weights/pallas_call | solution.py:309
  74.8 7.1 %near_weights.1 = (bf16[384,512]{1,0:T(8,128)(2,1)}, bf16[384,512]{1,0:T(8,128)(2,1)}, bf16[384,512]{1,0:T(8,128)(2,1)}, bf16[384,512]{1,0:T(8,128)(2,1)}, bf16[1152,1152]{1,0:T(8,128)(2,1)}) custom-call(s32[384,1]{1,0:T(8,128)S(1)} %copy-done.6, f32[4,384,128]{2,1,0:T(8,128)S(1)} %broadcast_in_dim.30.row_inv, f32[4,1,384]{2,1,0:T(1,128)S(1)} %fusion.3.col_inv, ...), custom_call_target="tpu_custom_call" | custom-call | flops 3623878656 | bytes 12582912 | tf_op jit(solution)/shard_map/near_weights/pallas_call | solution.py:309
  81.9 2.3 %collective-permute-start.12 = (bf16[384,512]{1,0:T(8,128)(2,1)}, bf16[384,512]{1,0:T(8,128)(2,1)}, u32[]{:S(2)}, u32[]{:S(2)}) collective-permute-start(bf16[384,512]{1,0:T(8,128)(2,1)} %get-tuple-element.57), channel_id=1, source_target_pairs={{0,3},{1,0},{2,1},{3,2},{16,17},{17,18},{18,19},{19,16},{4,7},{5,4... | collective-permute-start | bytes 1179656 | tf_op jit(solution)/shard_map/ppermute | solution.py:22
  84.1 3.6 %collective-permute-done.17.refs_7_ = bf16[384,512]{1,0:T(8,128)(2,1)S(1)} collective-permute-done((bf16[384,512]{1,0:T(8,128)(2,1)S(1)}, bf16[384,512]{1,0:T(8,128)(2,1)S(1)}, u32[]{:S(2)}, u32[]{:S(2)}) %collective-permute-start.17) | collective-permute-done | bytes 393248 | tf_op jit(solution)/shard_map/ppermute | solution.py:22
  94.9 4.0 %own_weights.1 = (f32[384,512]{1,0:T(8,128)S(1)}, f32[384,512]{1,0:T(8,128)S(1)}) custom-call(bf16[1152,1152]{1,0:T(8,128)(2,1)} %get-tuple-element.63.refs_0_, bf16[384,1536]{1,0:T(8,128)(2,1)S(1)} %get-tuple-element.55.wide.refs_1_, bf16[1536,384]{1,0:T(8,128)(2,1)S(1)} %copy-done.2, bf16[1152,512]{1,0:T(8,128)(2,1)} %get-tuple-element.51.rows_near.refs_0_.refs_3_, ...), custom_call_target="tpu_custom_call" | custom-call | flops 1207959552 | bytes 12582912 | tf_op jit(solution)/shard_map/own_weights/pallas_call | solution.py:309
  99.9 2.6 %row_gradients.1 = (bf16[384,1024]{1,0:T(8,128)(2,1)S(1)}, bf16[400,512]{1,0:T(8,128)(2,1)S(1)}, bf16[384,512]{1,0:T(8,128)(2,1)S(1)}) custom-call(f32[1]{0:T(128)S(6)} %copy.20.refs_1_.scale, s32[1]{0:T(128)} %bitcast.15.core, f32[1]{0:T(128)} %bitcast.16.ring_loss, f32[384,512]{1,0:T(8,128)S(1)} %get-tuple-element.66.by_row, ...), custom_call_target="tpu_custom_call" | custom-call | flops 150994944 | bytes 12582912 | tf_op jit(solution)/shard_map/row_gradients/pallas_call | solution.py:309
  106.3 2.9 %collective-permute-start.23 = (bf16[384,512]{1,0:T(8,128)(2,1)S(1)}, bf16[384,512]{1,0:T(8,128)(2,1)S(1)}, u32[]{:S(2)}, u32[]{:S(2)}) collective-permute-start(bf16[384,512]{1,0:T(8,128)(2,1)S(1)} %collective-permute-done.21.refs_3_), channel_id=1, source_target_pairs={{0,96},{32,0},{64,32},{96,64},{16,48},{48,80},{80,112},{112,16},{1... | collective-permute-start | bytes 1179656 | tf_op jit(solution)/shard_map/ppermute | solution.py:21
  109.3 8.6 %hidden_grad.1 = bf16[384,3584]{1,0:T(8,128)(2,1)} custom-call(bf16[384,1024]{1,0:T(8,128)(2,1)S(1)} %get-tuple-element.74.rows, bf16[3584,1024]{1,0:T(8,128)(2,1)} %weights.1), custom_call_target="tpu_custom_call" | custom-call | flops 2818572288 | bytes 11534336 | tf_op jit(solution)/shard_map/hidden_grad/pallas_call | solution.py:235
  117.8 4.6 %collective-permute-done.22.refs_4_ = bf16[384,512]{1,0:T(8,128)(2,1)S(1)} collective-permute-done((bf16[384,512]{1,0:T(8,128)(2,1)S(1)}, bf16[384,512]{1,0:T(8,128)(2,1)S(1)}, u32[]{:S(2)}, u32[]{:S(2)}) %collective-permute-start.22) | collective-permute-done | bytes 393248 | tf_op jit(solution)/shard_map/ppermute | solution.py:21
  125.1 5.5 %near_rows.1.first = f32[896,512]{1,0:T(8,128)S(1)} custom-call(s32[3]{0:T(128)S(1)} %pad_add_fusion.places, bf16[4,384,896]{2,1,0:T(8,128)(2,1)} %all-to-all-done.hidden_own, bf16[4,384,896]{2,1,0:T(8,128)(2,1)} %collective-permute-done.16.hidden_other, bf16[400,512]{1,0:T(8,128)(2,1)S(1)} %get-tuple-element.72.refs_0_.kept, ...), custom_call_target="tpu_custom_call" | custom-call | flops 21139292160 | bytes 8388608 | tf_op jit(solution)/shard_map/near_rows/pallas_call | solution.py:289
  130.6 2.6 %collective-permute-done.25.other_far = bf16[384,512]{1,0:T(8,128)(2,1)S(1)} collective-permute-done((bf16[384,512]{1,0:T(8,128)(2,1)S(1)}, bf16[384,512]{1,0:T(8,128)(2,1)S(1)}, u32[]{:S(2)}, u32[]{:S(2)}) %collective-permute-start.25) | collective-permute-done | bytes 393248 | tf_op jit(solution)/shard_map/ppermute | solution.py:21
  133.3 2.5 %last_rows.1 = bf16[32,32,512]{2,1,0:T(8,128)(2,1)S(1)} custom-call(s32[1]{0:T(128)} %bitcast.places, bf16[4,384,896]{2,1,0:T(8,128)(2,1)} %all-to-all-done.hidden_own, bf16[4,384,896]{2,1,0:T(8,128)(2,1)} %collective-permute-done.16.hidden_other, bf16[400,512]{1,0:T(8,128)(2,1)S(1)} %collective-permute-done.24.far, ...), custom_call_target="tpu_custom_call" | custom-call | flops 704643072 | bytes 8388608 | tf_op jit(solution)/shard_map/last_rows/pallas_call | solution.py:289
  135.8 22.6 %all_to_all.10 = bf16[32,32,512]{2,1,0:T(8,128)(2,1)S(1)} all-to-all(bf16[32,32,512]{2,1,0:T(8,128)(2,1)S(1)} %last_rows.1), channel_id=1, replica_groups=mesh['y'=4,'core'=2,'z'=4,'x'=4] {'core','z','x'}, dimensions={0} | all-to-all | bytes 2097152 | tf_op jit(solution)/shard_map/all_to_all | solution.py:424
  (114 shorter events, 40.8 us)
Async XLA Ops:
  8.4 16.4 %collective-permute-start = (bf16[384,1024]{1,0:T(8,128)(2,1)S(1)}, bf16[384,1024]{1,0:T(8,128)(2,1)S(1)}, u32[]{:S(2)}, u32[]{:S(2)}) collective-permute-start(bf16[384,1024]{1,0:T(8,128)(2,1)S(1)} %get-tuple-element.79.refs_3_.refs_6_.refs_7_), channel_id=1, source_target_pairs={{0,1},{1,2},{2,3},{3,0},{16,19},{17,16},{18,17},{19,18},{4,5},{5,6... | collective-permute-start | bytes 2359304 | tf_op jit(solution)/shard_map/ppermute | solution.py:22
  9.9 19.7 %collective-permute-start.2 = (bf16[384,1024]{1,0:T(8,128)(2,1)S(1)}, bf16[384,1024]{1,0:T(8,128)(2,1)}, u32[]{:S(2)}, u32[]{:S(2)}) collective-permute-start(bf16[384,1024]{1,0:T(8,128)(2,1)S(1)} %get-tuple-element.79.refs_3_.refs_6_.refs_7_), channel_id=1, source_target_pairs={{0,4},{4,8},{8,12},{12,0},{16,28},{20,16},{24,20},{28,24},{1,5},{5... | collective-permute-start | bytes 2359304 | tf_op jit(solution)/shard_map/ppermute | solution.py:22
  11.8 21.3 %collective-permute-start.1 = (bf16[384,1024]{1,0:T(8,128)(2,1)S(1)}, bf16[384,1024]{1,0:T(8,128)(2,1)S(1)}, u32[]{:S(2)}, u32[]{:S(2)}) collective-permute-start(bf16[384,1024]{1,0:T(8,128)(2,1)S(1)} %get-tuple-element.79.refs_3_.refs_6_.refs_7_), channel_id=1, source_target_pairs={{0,3},{1,0},{2,1},{3,2},{16,17},{17,18},{18,19},{19,16},{4,7},{5,4... | collective-permute-start | bytes 2359304 | tf_op jit(solution)/shard_map/ppermute | solution.py:22
  13.6 20.5 %collective-permute-start.3 = (bf16[384,1024]{1,0:T(8,128)(2,1)S(1)}, bf16[384,1024]{1,0:T(8,128)(2,1)S(1)}, u32[]{:S(2)}, u32[]{:S(2)}) collective-permute-start(bf16[384,1024]{1,0:T(8,128)(2,1)S(1)} %get-tuple-element.79.refs_3_.refs_6_.refs_7_), channel_id=1, source_target_pairs={{0,12},{4,0},{8,4},{12,8},{16,20},{20,24},{24,28},{28,16},{1,13},{... | collective-permute-start | bytes 2359304 | tf_op jit(solution)/shard_map/ppermute | solution.py:22
  17.7 52.6 %all-to-all-start = ((bf16[4,384,896]{2,1,0:T(8,128)(2,1)}), bf16[4,384,896]{2,1,0:T(8,128)(2,1)}, u32[]{:S(2)}, u32[]{:S(2)}) async-start(bf16[4,384,896]{2,1,0:T(8,128)(2,1)} %pad_maximum_fusion), calls=%async_computation | async-start | bytes 5505024 | tf_op jit(solution)/shard_map/all_to_all | solution.py:348
  24.7 21.5 %collective-permute-start.4 = (bf16[384,1024]{1,0:T(8,128)(2,1)S(1)}, bf16[384,1024]{1,0:T(8,128)(2,1)}, u32[]{:S(2)}, u32[]{:S(2)}) collective-permute-start(bf16[384,1024]{1,0:T(8,128)(2,1)S(1)} %collective-permute-done.refs_4_), channel_id=1, source_target_pairs={{0,1},{1,2},{2,3},{3,0},{16,19},{17,16},{18,17},{19,18},{4,5},{5,6... | collective-permute-start | bytes 2359304 | tf_op jit(solution)/shard_map/ppermute | solution.py:22
  29.6 16.7 %collective-permute-start.5 = (bf16[384,1024]{1,0:T(8,128)(2,1)}, bf16[384,1024]{1,0:T(8,128)(2,1)}, u32[]{:S(2)}, u32[]{:S(2)}) collective-permute-start(bf16[384,1024]{1,0:T(8,128)(2,1)} %collective-permute-done.2.refs_7_.refs_8_), channel_id=1, source_target_pairs={{0,4},{4,8},{8,12},{12,0},{16,28},{20,16},{24,20},{28,24},{1,5},{5... | collective-permute-start | bytes 2359304 | tf_op jit(solution)/shard_map/ppermute | solution.py:22
  55.1 10.6 %collective-permute-start.10 = (f32[4,384]{1,0:T(4,128)S(1)}, f32[4,384]{1,0:T(4,128)S(1)}, u32[]{:S(2)}, u32[]{:S(2)}) collective-permute-start(f32[4,384]{1,0:T(4,128)S(1)} %add_reduce_fusion.1), channel_id=1, source_target_pairs={{0,8},{4,12},{8,0},{12,4},{16,24},{20,28},{24,16},{28,20},{1,9},{5... | collective-permute-start | bytes 18440 | tf_op jit(solution)/shard_map/ppermute | solution.py:22
  59.0 5.8 %collective-permute-start.9 = (f32[4,384]{1,0:T(4,128)S(1)}, f32[4,384]{1,0:T(4,128)S(1)}, u32[]{:S(2)}, u32[]{:S(2)}) collective-permute-start(f32[4,384]{1,0:T(4,128)S(1)} %add_reduce_fusion.1), channel_id=1, source_target_pairs={{0,12},{4,0},{8,4},{12,8},{16,20},{20,24},{24,28},{28,16},{1,13},{... | collective-permute-start | bytes 18440 | tf_op jit(solution)/shard_map/ppermute | solution.py:22
  59.9 5.8 %collective-permute-start.11 = (f32[4,384]{1,0:T(4,128)S(1)}, f32[4,384]{1,0:T(4,128)S(1)}, u32[]{:S(2)}, u32[]{:S(2)}) collective-permute-start(f32[4,384]{1,0:T(4,128)S(1)} %add_reduce_fusion.1), channel_id=1, source_target_pairs={{0,4},{4,8},{8,12},{12,0},{16,28},{20,16},{24,20},{28,24},{1,5},{5... | collective-permute-start | bytes 18440 | tf_op jit(solution)/shard_map/ppermute | solution.py:22
  61.4 8.2 %collective-permute-start.7 = (f32[4,512]{1,0:T(4,128)S(1)}, f32[4,512]{1,0:T(4,128)S(1)}, u32[]{:S(2)}, u32[]{:S(2)}) collective-permute-start(f32[4,512]{1,0:T(4,128)S(1)} %pad_maximum_fusion.2), channel_id=1, source_target_pairs={{0,2},{1,3},{2,0},{3,1},{16,18},{17,19},{18,16},{19,17},{4,6},{5,7... | collective-permute-start | bytes 24584 | tf_op jit(solution)/shard_map/ppermute | solution.py:22
  70.6 29.4 %collective-permute-start.16 = (bf16[4,384,896]{2,1,0:T(8,128)(2,1)}, bf16[4,384,896]{2,1,0:T(8,128)(2,1)}, u32[]{:S(2)}, u32[]{:S(2)}) collective-permute-start(bf16[4,384,896]{2,1,0:T(8,128)(2,1)} %all-to-all-done.hidden_own), channel_id=1, source_target_pairs={{0,16},{16,0},{1,17},{17,1},{2,18},{18,2},{3,19},{19,3},{4,20},{20... | collective-permute-start | bytes 8257544 | tf_op jit(solution)/shard_map/ppermute | solution.py:26
  74.3 13.5 %collective-permute-start.17 = (bf16[384,512]{1,0:T(8,128)(2,1)S(1)}, bf16[384,512]{1,0:T(8,128)(2,1)S(1)}, u32[]{:S(2)}, u32[]{:S(2)}) collective-permute-start(bf16[384,512]{1,0:T(8,128)(2,1)S(1)} %get-tuple-element.64), channel_id=1, source_target_pairs={{0,2},{1,3},{2,0},{3,1},{16,18},{17,19},{18,16},{19,17},{4,6},{5,7... | collective-permute-start | bytes 1179656 | tf_op jit(solution)/shard_map/ppermute | solution.py:22
  74.3 15.5 %collective-permute-start.18 = (bf16[384,512]{1,0:T(8,128)(2,1)S(1)}, bf16[384,512]{1,0:T(8,128)(2,1)S(1)}, u32[]{:S(2)}, u32[]{:S(2)}) collective-permute-start(bf16[384,512]{1,0:T(8,128)(2,1)S(1)} %get-tuple-element.65), channel_id=1, source_target_pairs={{0,8},{4,12},{8,0},{12,4},{16,24},{20,28},{24,16},{28,20},{1,9},{5... | collective-permute-start | bytes 1179656 | tf_op jit(solution)/shard_map/ppermute | solution.py:22
  81.9 17.0 %collective-permute-start.12 = (bf16[384,512]{1,0:T(8,128)(2,1)}, bf16[384,512]{1,0:T(8,128)(2,1)}, u32[]{:S(2)}, u32[]{:S(2)}) collective-permute-start(bf16[384,512]{1,0:T(8,128)(2,1)} %get-tuple-element.57), channel_id=1, source_target_pairs={{0,3},{1,0},{2,1},{3,2},{16,17},{17,18},{18,19},{19,16},{4,7},{5,4... | collective-permute-start | bytes 1179656 | tf_op jit(solution)/shard_map/ppermute | solution.py:22
  84.1 14.8 %collective-permute-start.13 = (bf16[384,512]{1,0:T(8,128)(2,1)}, bf16[384,512]{1,0:T(8,128)(2,1)}, u32[]{:S(2)}, u32[]{:S(2)}) collective-permute-start(bf16[384,512]{1,0:T(8,128)(2,1)} %get-tuple-element.58), channel_id=1, source_target_pairs={{0,1},{1,2},{2,3},{3,0},{16,19},{17,16},{18,17},{19,18},{4,5},{5,6... | collective-permute-start | bytes 1179656 | tf_op jit(solution)/shard_map/ppermute | solution.py:22
  87.8 11.8 %collective-permute-start.14 = (bf16[384,512]{1,0:T(8,128)(2,1)}, bf16[384,512]{1,0:T(8,128)(2,1)}, u32[]{:S(2)}, u32[]{:S(2)}) collective-permute-start(bf16[384,512]{1,0:T(8,128)(2,1)} %get-tuple-element.59), channel_id=1, source_target_pairs={{0,12},{4,0},{8,4},{12,8},{16,20},{20,24},{24,28},{28,16},{1,13},{... | collective-permute-start | bytes 1179656 | tf_op jit(solution)/shard_map/ppermute | solution.py:22
  90.6 9.3 %collective-permute-start.15 = (bf16[384,512]{1,0:T(8,128)(2,1)}, bf16[384,512]{1,0:T(8,128)(2,1)}, u32[]{:S(2)}, u32[]{:S(2)}) collective-permute-start(bf16[384,512]{1,0:T(8,128)(2,1)} %get-tuple-element.60), channel_id=1, source_target_pairs={{0,4},{4,8},{8,12},{12,0},{16,28},{20,16},{24,20},{28,24},{1,5},{5... | collective-permute-start | bytes 1179656 | tf_op jit(solution)/shard_map/ppermute | solution.py:22
  102.6 15.2 %collective-permute-start.19 = (bf16[400,512]{1,0:T(8,128)(2,1)S(1)}, bf16[400,512]{1,0:T(8,128)(2,1)S(1)}, u32[]{:S(2)}, u32[]{:S(2)}) collective-permute-start(bf16[400,512]{1,0:T(8,128)(2,1)S(1)} %get-tuple-element.72.refs_0_.kept), channel_id=1, source_target_pairs={{0,32},{32,64},{64,96},{96,0},{16,112},{48,16},{80,48},{112,80},{1... | collective-permute-start | bytes 1228808 | tf_op jit(solution)/shard_map/ppermute | solution.py:21
  104.3 19.9 %collective-permute-start.20 = (bf16[400,512]{1,0:T(8,128)(2,1)S(1)}, bf16[400,512]{1,0:T(8,128)(2,1)S(1)}, u32[]{:S(2)}, u32[]{:S(2)}) collective-permute-start(bf16[400,512]{1,0:T(8,128)(2,1)S(1)} %get-tuple-element.72.refs_0_.kept), channel_id=1, source_target_pairs={{0,96},{32,0},{64,32},{96,64},{16,48},{48,80},{80,112},{112,16},{1... | collective-permute-start | bytes 1228808 | tf_op jit(solution)/shard_map/ppermute | solution.py:21
  105.9 16.5 %collective-permute-start.22 = (bf16[384,512]{1,0:T(8,128)(2,1)S(1)}, bf16[384,512]{1,0:T(8,128)(2,1)S(1)}, u32[]{:S(2)}, u32[]{:S(2)}) collective-permute-start(bf16[384,512]{1,0:T(8,128)(2,1)S(1)} %collective-permute-done.21.refs_3_), channel_id=1, source_target_pairs={{0,32},{32,64},{64,96},{96,0},{16,112},{48,16},{80,48},{112,80},{1... | collective-permute-start | bytes 1179656 | tf_op jit(solution)/shard_map/ppermute | solution.py:21
  106.3 18.8 %collective-permute-start.23 = (bf16[384,512]{1,0:T(8,128)(2,1)S(1)}, bf16[384,512]{1,0:T(8,128)(2,1)S(1)}, u32[]{:S(2)}, u32[]{:S(2)}) collective-permute-start(bf16[384,512]{1,0:T(8,128)(2,1)S(1)} %collective-permute-done.21.refs_3_), channel_id=1, source_target_pairs={{0,96},{32,0},{64,32},{96,64},{16,48},{48,80},{80,112},{112,16},{1... | collective-permute-start | bytes 1179656 | tf_op jit(solution)/shard_map/ppermute | solution.py:21
  117.8 12.8 %collective-permute-start.24 = (bf16[400,512]{1,0:T(8,128)(2,1)S(1)}, bf16[400,512]{1,0:T(8,128)(2,1)S(1)}, u32[]{:S(2)}, u32[]{:S(2)}) collective-permute-start(bf16[400,512]{1,0:T(8,128)(2,1)S(1)} %collective-permute-done.19.refs_1_.back), channel_id=1, source_target_pairs={{0,32},{32,64},{64,96},{96,0},{16,112},{48,16},{80,48},{112,80},{1... | collective-permute-start | bytes 1228808 | tf_op jit(solution)/shard_map/ppermute | solution.py:21
  122.4 10.9 %collective-permute-start.25 = (bf16[384,512]{1,0:T(8,128)(2,1)S(1)}, bf16[384,512]{1,0:T(8,128)(2,1)S(1)}, u32[]{:S(2)}, u32[]{:S(2)}) collective-permute-start(bf16[384,512]{1,0:T(8,128)(2,1)S(1)} %collective-permute-done.22.refs_4_), channel_id=1, source_target_pairs={{0,32},{32,64},{64,96},{96,0},{16,112},{48,16},{80,48},{112,80},{1... | collective-permute-start | bytes 1179656 | tf_op jit(solution)/shard_map/ppermute | solution.py:21
  (20 other events, 110.6 us)

commit v3 on v2

--- a/solution.py
+++ b/solution.py
@@ -282,6 +282,58 @@
         out[k, size:] = spare
 
 
+def unit_kernel(hidden, left, right, unit_rows, unit_low, lengths, total):
+    step = pl.program_id(0)
+    half = left.shape[1]
+
+    @pl.when(step == 0)
+    def _():
+        total[...] = jnp.zeros_like(total)
+
+    total[:, :half] += product(hidden[...], left[...])
+    total[:, half:] += product(hidden[...], right[...])
+
+    @pl.when(step == pl.num_programs(0) - 1)
+    def _():
+        projected = total[...]
+        length = jnp.sqrt(jnp.sum(projected * projected, axis=1, keepdims=True) + epsilon)
+        units = projected / length
+        lengths[...] = length
+        unit_rows[...] = units
+        unit_low[...] = units.astype(unit_low.dtype)
+
+
+def unit_vectors(hidden, projection, steps=7):
+    rows, depth = hidden.shape
+    width = projection.shape[1]
+    block = depth // steps
+    return pl.pallas_call(
+        unit_kernel,
+        grid=(steps,),
+        out_shape=(
+            jax.ShapeDtypeStruct((rows, width), jnp.float32),
+            jax.ShapeDtypeStruct((rows, width), jnp.bfloat16),
+            jax.ShapeDtypeStruct((rows, 1), jnp.float32),
+        ),
+        in_specs=[
+            pl.BlockSpec((rows, block), lambda i: (0, i)),
+            pl.BlockSpec((block, width // 2), lambda i: (i, 0)),
+            pl.BlockSpec((block, width // 2), lambda i: (i, 1)),
+        ],
+        out_specs=(
+            pl.BlockSpec((rows, width), lambda i: (0, 0)),
+            pl.BlockSpec((rows, width), lambda i: (0, 0)),
+            pl.BlockSpec((rows, 1), lambda i: (0, 0)),
+        ),
+        scratch_shapes=[pltpu.VMEM((rows, width), jnp.float32)],
+        compiler_params=pltpu.CompilerParams(vmem_limit_bytes=48 << 20),
+        cost_estimate=pl.CostEstimate(
+            flops=2 * rows * width * depth, transcendentals=0, bytes_accessed=12 << 20
+        ),
+        name="unit_vectors",
+    )(hidden, projection, projection)
+
+
 def call_by_place(kernel, name, flops, places, hidden_own, hidden_other, inputs, out_shape, scratch=()):
     block = pl.BlockSpec((1,) + hidden_own.shape[1:], lambda i, places: (places[i], 0, 0))
     def all_of(shape):
@@ -335,11 +387,7 @@
     active = (jnp.any(apart[:, None] == offsets[None, :], axis=1) | (apart == 0)).astype(jnp.int32)
     pos = (positives % rows)[:, None]
 
-    projected = jnp.dot(hidden, projection, preferred_element_type=jnp.float32)
-    lengths = jnp.sqrt(jnp.sum(projected * projected, axis=1, keepdims=True) + epsilon)
-    unit_rows = projected / lengths
-    unit_low = unit_rows.astype(jnp.bfloat16)
-
+    unit_rows, unit_low, lengths = unit_vectors(hidden, projection)
     x_back, x_far, x_ahead = ring_gather(unit_low, "x")
     z_back, z_far, z_ahead = ring_gather(unit_low, "z")
 

time: 162 us -> 163 us (level)
  Pallas kernels: 48.1 us -> 56.1 us
  matrix products: 6.26 us -> 0 us
  waiting for transfers between devices: 22 us -> 23.9 us
    pallas_call x0 -> x1, Pallas kernels: none -> 7.68 us  [unit_vectors(): pl.pallas_call(unit_kernel, grid=(steps,), out_shape=(jax.ShapeDtypeStruc...]
    dot_general x1 -> x0, matrix products: 6.26 us -> none  [per_device(): projected = jnp.dot(hidden, projection, preferred_element_type=jnp.float32)]
    ppermute x18, waiting for transfers between devices: 13.9 us -> 15.7 us  [send(): lax.ppermute(array, ('core', axis), [(4 * core + i, 4 * core + j) for cor...]
    unnamed x34 -> x30, local copies, waits for them, and re-layouts: 9.35 us -> 8.07 us
  transfers between devices with their start and end apart: 27 -> 27, of which waited for: 10 -> 12; matrix products, arithmetic and copies ran while one was open for 3% -> 3% of each run, Pallas kernels for 27% -> 27%
where the time goes in v3:
time: 163 us; the launch traced here: 162 us
  Pallas kernels  56.1 us (34%)
  starting transfers between devices  38.2 us (23%)
  waiting for transfers between devices  23.9 us (15%)
  blocking collectives  23.6 us (14%)
  local copies, waits for them, and re-layouts  8.86 us (5%)
  other arithmetic  6.44 us (4%)
  between operations  4.7 us (3%)
    ppermute x18, starting transfers between devices, send(): lax.ppermute(array, ('core', axis), [(4 * core + i, 4 * core + j) for cor...  25.1 us
    all_to_all x1, blocking collectives, per_device(): arrived = lax.all_to_all(part, ('core', 'z', 'x'), 0, 0).astype(jnp.float32)  23.6 us
    pallas_call x4, Pallas kernels, call(): pl.pallas_call(kernel, out_shape=out_shape, in_specs=[smem] * scalars + [...  17.2 us
    ppermute x18, waiting for transfers between devices, send(): lax.ppermute(array, ('core', axis), [(4 * core + i, 4 * core + j) for cor...  15.7 us
    pallas_call x2, Pallas kernels, score_tiles(): pl.pallas_call(functools.partial(score_kernel, tiles, names, pieces, fina...  14.7 us
    pallas_call x1, Pallas kernels, hidden_grad(): pl.pallas_call(hidden_kernel, grid=(steps,), out_shape=jax.ShapeDtypeStru...  8.58 us
    ppermute x6, starting transfers between devices, send(): lax.ppermute(array, ('y', 'core'), [(2 * i + core, 2 * j + core) for core...  8.29 us
    ppermute x6, waiting for transfers between devices, send(): lax.ppermute(array, ('y', 'core'), [(2 * i + core, 2 * j + core) for core...  8.17 us
  transfers between devices with their start and end apart: 27, of which 12 were waited for; matrix products, arithmetic and copies ran while one was open for 3% of the time, Pallas kernels for 27%

profile of v3, /device:TPU:0, one launch (start us, length us, event | category | flops | bytes accessed | tf_op | source)
XLA Modules:
  0.0 161.8 jit_solution(6927996778602816781)
XLA Ops:
  2.4 7.7 %unit_vectors.1 = (f32[384,1024]{1,0:T(8,128)S(1)}, bf16[384,1024]{1,0:T(8,128)(2,1)S(1)}, f32[384,1]{1,0:T(8,128)S(1)}) custom-call(bf16[384,3584]{1,0:T(8,128)(2,1)S(1)} %copy-done, bf16[3584,1024]{1,0:T(8,128)(2,1)} %weights.1, bf16[3584,1024]{1,0:T(8,128)(2,1)} %weights.1), custom_call_target="tpu_custom_call" | custom-call | flops 2818572288 | bytes 12582912 | tf_op jit(solution)/shard_map/unit_vectors/pallas_call | solution.py:310
  10.1 4.2 %collective-permute-start.3 = (bf16[384,1024]{1,0:T(8,128)(2,1)S(1)}, bf16[384,1024]{1,0:T(8,128)(2,1)S(1)}, u32[]{:S(2)}, u32[]{:S(2)}) collective-permute-start(bf16[384,1024]{1,0:T(8,128)(2,1)S(1)} %get-tuple-element.44.refs_3_.refs_6_.refs_7_), channel_id=1, source_target_pairs={{0,12},{4,0},{8,4},{12,8},{16,20},{20,24},{24,28},{28,16},{1,13},{... | collective-permute-start | bytes 2359304 | tf_op jit(solution)/shard_map/ppermute | solution.py:22
  14.3 2.8 %collective-permute-start.1 = (bf16[384,1024]{1,0:T(8,128)(2,1)S(1)}, bf16[384,1024]{1,0:T(8,128)(2,1)S(1)}, u32[]{:S(2)}, u32[]{:S(2)}) collective-permute-start(bf16[384,1024]{1,0:T(8,128)(2,1)S(1)} %get-tuple-element.44.refs_3_.refs_6_.refs_7_), channel_id=1, source_target_pairs={{0,3},{1,0},{2,1},{3,2},{16,17},{17,18},{18,19},{19,16},{4,7},{5,4... | collective-permute-start | bytes 2359304 | tf_op jit(solution)/shard_map/ppermute | solution.py:22
  19.1 4.7 %all-to-all-start = ((bf16[4,384,896]{2,1,0:T(8,128)(2,1)}), bf16[4,384,896]{2,1,0:T(8,128)(2,1)}, u32[]{:S(2)}, u32[]{:S(2)}) async-start(bf16[4,384,896]{2,1,0:T(8,128)(2,1)} %pad_maximum_fusion), calls=%async_computation | async-start | bytes 5505024 | tf_op jit(solution)/shard_map/all_to_all | solution.py:396
  23.9 8.0 %collective-permute-done.2.refs_7_.refs_8_ = bf16[384,1024]{1,0:T(8,128)(2,1)} collective-permute-done((bf16[384,1024]{1,0:T(8,128)(2,1)S(1)}, bf16[384,1024]{1,0:T(8,128)(2,1)}, u32[]{:S(2)}, u32[]{:S(2)}) %collective-permute-start.2) | collective-permute-done | bytes 786464 | tf_op jit(solution)/shard_map/ppermute | solution.py:22
  32.0 2.7 %collective-permute-done.refs_4_ = bf16[384,1024]{1,0:T(8,128)(2,1)} collective-permute-done((bf16[384,1024]{1,0:T(8,128)(2,1)S(1)}, bf16[384,1024]{1,0:T(8,128)(2,1)}, u32[]{:S(2)}, u32[]{:S(2)}) %collective-permute-start) | collective-permute-done | bytes 786464 | tf_op jit(solution)/shard_map/ppermute | solution.py:22
  38.2 7.9 %scores.2 = (bf16[9,384,384]{2,1,0:T(8,128)(2,1)}, f32[4,384,128]{2,1,0:T(8,128)S(1)}, f32[4,8,384]{2,1,0:T(8,128)S(1)}, bf16[1152,512]{1,0:T(8,128)(2,1)}, bf16...) custom-call(s32[16]{0:T(128)S(1)} %or_convert_fusion.refs_0_, f32[1]{0:T(128)S(6)} %copy.18.refs_1_.scale, ...), custom_call_target="tpu_custom_call" | custom-call | flops 2717908992 | bytes 16777216 | tf_op jit(solution)/shard_map/scores/pallas_call | solution.py:112
  49.4 6.8 %scores.3 = (bf16[7,384,384]{2,1,0:T(8,128)(2,1)}, f32[4,384,128]{2,1,0:T(8,128)S(1)}, f32[4,8,384]{2,1,0:T(8,128)S(1)}, bf16[384,512]{1,0:T(8,128)(2,1)S(1)}, b...) custom-call(s32[16]{0:T(128)S(1)} %or_convert_fusion.refs_0_, f32[1]{0:T(128)S(6)} %copy.18.refs_1_.scale, ...), custom_call_target="tpu_custom_call" | custom-call | flops 2113929216 | bytes 16777216 | tf_op jit(solution)/shard_map/scores/pallas_call | solution.py:112
  56.3 3.1 %collective-permute-start.10 = (f32[4,384]{1,0:T(4,128)S(1)}, f32[4,384]{1,0:T(4,128)S(1)}, u32[]{:S(2)}, u32[]{:S(2)}) collective-permute-start(f32[4,384]{1,0:T(4,128)S(1)} %add_reduce_fusion.1), channel_id=1, source_target_pairs={{0,8},{4,12},{8,0},{12,4},{16,24},{20,28},{24,16},{28,20},{1,9},{5... | collective-permute-start | bytes 18440 | tf_op jit(solution)/shard_map/ppermute | solution.py:22
  60.8 2.2 %collective-permute-start.7 = (f32[4,512]{1,0:T(4,128)S(1)}, f32[4,512]{1,0:T(4,128)S(1)}, u32[]{:S(2)}, u32[]{:S(2)}) collective-permute-start(f32[4,512]{1,0:T(4,128)S(1)} %pad_maximum_fusion.2), channel_id=1, source_target_pairs={{0,2},{1,3},{2,0},{3,1},{16,18},{17,19},{18,16},{19,17},{4,6},{5,7... | collective-permute-start | bytes 24584 | tf_op jit(solution)/shard_map/ppermute | solution.py:22
  63.8 2.3 %collective-permute-start.6 = (f32[4,512]{1,0:T(4,128)S(1)}, f32[4,512]{1,0:T(4,128)S(1)}, u32[]{:S(2)}, u32[]{:S(2)}) collective-permute-start(f32[4,512]{1,0:T(4,128)S(1)} %pad_maximum_fusion.2), channel_id=1, source_target_pairs={{0,3},{1,0},{2,1},{3,2},{16,17},{17,18},{18,19},{19,16},{4,7},{5,4... | collective-permute-start | bytes 24584 | tf_op jit(solution)/shard_map/ppermute | solution.py:22
  68.8 3.6 %far_weights.1 = (bf16[384,512]{1,0:T(8,128)(2,1)S(1)}, bf16[384,512]{1,0:T(8,128)(2,1)S(1)}, bf16[384,1536]{1,0:T(8,128)(2,1)S(1)}, bf16[1536,384]{1,0:T(8,128)(2,1)S(1)}) custom-call(f32[4,384,128]{2,1,0:T(8,128)S(1)} %broadcast_in_dim.29.row_inv, f32[4,1,384]{2,1,0:T(1,128)S(1)} %fusion.3.col_inv, bf16[7,384,384]{2,1,0:T(8,128)(2,1)} %get-tuple-element.54.far, ...), custom_call_target="tpu_custom_call" | custom-call | flops 1207959552 | bytes 12582912 | tf_op jit(solution)/shard_map/far_weights/pallas_call | solution.py:361
  72.4 1.8 %collective-permute-start.17 = (bf16[384,512]{1,0:T(8,128)(2,1)S(1)}, bf16[384,512]{1,0:T(8,128)(2,1)S(1)}, u32[]{:S(2)}, u32[]{:S(2)}) collective-permute-start(bf16[384,512]{1,0:T(8,128)(2,1)S(1)} %get-tuple-element.68), channel_id=1, source_target_pairs={{0,2},{1,3},{2,0},{3,1},{16,18},{17,19},{18,16},{19,17},{4,6},{5,7... | collective-permute-start | bytes 1179656 | tf_op jit(solution)/shard_map/ppermute | solution.py:22
  74.2 1.9 %collective-permute-start.18 = (bf16[384,512]{1,0:T(8,128)(2,1)S(1)}, bf16[384,512]{1,0:T(8,128)(2,1)S(1)}, u32[]{:S(2)}, u32[]{:S(2)}) collective-permute-start(bf16[384,512]{1,0:T(8,128)(2,1)S(1)} %get-tuple-element.69), channel_id=1, source_target_pairs={{0,8},{4,12},{8,0},{12,4},{16,24},{20,28},{24,16},{28,20},{1,9},{5... | collective-permute-start | bytes 1179656 | tf_op jit(solution)/shard_map/ppermute | solution.py:22
  76.1 7.2 %near_weights.1 = (bf16[384,512]{1,0:T(8,128)(2,1)}, bf16[384,512]{1,0:T(8,128)(2,1)}, bf16[384,512]{1,0:T(8,128)(2,1)}, bf16[384,512]{1,0:T(8,128)(2,1)}, bf16[1152,1152]{1,0:T(8,128)(2,1)}) custom-call(s32[384,1]{1,0:T(8,128)S(1)} %broadcast_in_dim.32.refs_2_.pos, f32[4,384,128]{2,1,0:T(8,128)S(1)} %broadcast_in_dim.29.row_inv, ...), custom_call_target="tpu_custom_call" | custom-call | flops 3623878656 | bytes 12582912 | tf_op jit(solution)/shard_map/near_weights/pallas_call | solution.py:361
  91.0 4.0 %own_weights.1 = (f32[384,512]{1,0:T(8,128)S(1)}, f32[384,512]{1,0:T(8,128)S(1)}) custom-call(bf16[1152,1152]{1,0:T(8,128)(2,1)} %get-tuple-element.67.refs_0_, bf16[384,1536]{1,0:T(8,128)(2,1)S(1)} %get-tuple-element.59.wide.refs_1_, bf16[1536,384]{1,0:T(8,128)(2,1)S(1)} %copy-done.4, bf16[1152,512]{1,0:T(8,128)(2,1)} %get-tuple-element.55.rows_near.refs_0_.refs_3_, ...), custom_call_target="tpu_custom_call" | custom-call | flops 1207959552 | bytes 12582912 | tf_op jit(solution)/shard_map/own_weights/pallas_call | solution.py:361
  99.4 2.4 %row_gradients.1 = (bf16[384,1024]{1,0:T(8,128)(2,1)S(1)}, bf16[400,512]{1,0:T(8,128)(2,1)S(1)}, bf16[384,512]{1,0:T(8,128)(2,1)S(1)}) custom-call(f32[1]{0:T(128)S(6)} %copy.18.refs_1_.scale, s32[1]{0:T(128)} %bitcast.15.core, f32[1]{0:T(128)} %bitcast.16.ring_loss, f32[384,512]{1,0:T(8,128)S(1)} %get-tuple-element.70.by_row, ...), custom_call_target="tpu_custom_call" | custom-call | flops 150994944 | bytes 12582912 | tf_op jit(solution)/shard_map/row_gradients/pallas_call | solution.py:361
  105.5 2.9 %collective-permute-start.23 = (bf16[384,512]{1,0:T(8,128)(2,1)S(1)}, bf16[384,512]{1,0:T(8,128)(2,1)S(1)}, u32[]{:S(2)}, u32[]{:S(2)}) collective-permute-start(bf16[384,512]{1,0:T(8,128)(2,1)S(1)} %collective-permute-done.21.refs_3_), channel_id=1, source_target_pairs={{0,96},{32,0},{64,32},{96,64},{16,48},{48,80},{80,112},{112,16},{1... | collective-permute-start | bytes 1179656 | tf_op jit(solution)/shard_map/ppermute | solution.py:21
  108.5 8.6 %hidden_grad.1 = bf16[384,3584]{1,0:T(8,128)(2,1)} custom-call(bf16[384,1024]{1,0:T(8,128)(2,1)S(1)} %get-tuple-element.80.rows, bf16[3584,1024]{1,0:T(8,128)(2,1)} %weights.1), custom_call_target="tpu_custom_call" | custom-call | flops 2818572288 | bytes 11534336 | tf_op jit(solution)/shard_map/hidden_grad/pallas_call | solution.py:235
  117.1 4.6 %collective-permute-done.22.refs_4_ = bf16[384,512]{1,0:T(8,128)(2,1)S(1)} collective-permute-done((bf16[384,512]{1,0:T(8,128)(2,1)S(1)}, bf16[384,512]{1,0:T(8,128)(2,1)S(1)}, u32[]{:S(2)}, u32[]{:S(2)}) %collective-permute-start.22) | collective-permute-done | bytes 393248 | tf_op jit(solution)/shard_map/ppermute | solution.py:21
  124.3 5.5 %near_rows.1.first = f32[896,512]{1,0:T(8,128)S(1)} custom-call(s32[3]{0:T(128)S(1)} %pad_add_fusion.places, bf16[4,384,896]{2,1,0:T(8,128)(2,1)} %all-to-all-done.hidden_own, bf16[4,384,896]{2,1,0:T(8,128)(2,1)} %collective-permute-done.16.hidden_other, bf16[400,512]{1,0:T(8,128)(2,1)S(1)} %get-tuple-element.78.refs_0_.kept, ...), custom_call_target="tpu_custom_call" | custom-call | flops 21139292160 | bytes 8388608 | tf_op jit(solution)/shard_map/near_rows/pallas_call | solution.py:341
  129.9 2.6 %collective-permute-done.25.other_far = bf16[384,512]{1,0:T(8,128)(2,1)S(1)} collective-permute-done((bf16[384,512]{1,0:T(8,128)(2,1)S(1)}, bf16[384,512]{1,0:T(8,128)(2,1)S(1)}, u32[]{:S(2)}, u32[]{:S(2)}) %collective-permute-start.25) | collective-permute-done | bytes 393248 | tf_op jit(solution)/shard_map/ppermute | solution.py:21
  132.5 2.5 %last_rows.1 = bf16[32,32,512]{2,1,0:T(8,128)(2,1)S(1)} custom-call(s32[1]{0:T(128)} %bitcast.places, bf16[4,384,896]{2,1,0:T(8,128)(2,1)} %all-to-all-done.hidden_own, bf16[4,384,896]{2,1,0:T(8,128)(2,1)} %collective-permute-done.16.hidden_other, bf16[400,512]{1,0:T(8,128)(2,1)S(1)} %collective-permute-done.24.far, ...), custom_call_target="tpu_custom_call" | custom-call | flops 704643072 | bytes 8388608 | tf_op jit(solution)/shard_map/last_rows/pallas_call | solution.py:341
  135.0 23.6 %all_to_all.10 = bf16[32,32,512]{2,1,0:T(8,128)(2,1)S(1)} all-to-all(bf16[32,32,512]{2,1,0:T(8,128)(2,1)S(1)} %last_rows.1), channel_id=1, replica_groups=mesh['y'=4,'core'=2,'z'=4,'x'=4] {'core','z','x'}, dimensions={0} | all-to-all | bytes 2097152 | tf_op jit(solution)/shard_map/all_to_all | solution.py:472
  (107 shorter events, 33.6 us)
Async XLA Ops:
  10.1 25.9 %collective-permute-start.3 = (bf16[384,1024]{1,0:T(8,128)(2,1)S(1)}, bf16[384,1024]{1,0:T(8,128)(2,1)S(1)}, u32[]{:S(2)}, u32[]{:S(2)}) collective-permute-start(bf16[384,1024]{1,0:T(8,128)(2,1)S(1)} %get-tuple-element.44.refs_3_.refs_6_.refs_7_), channel_id=1, source_target_pairs={{0,12},{4,0},{8,4},{12,8},{16,20},{20,24},{24,28},{28,16},{1,13},{... | collective-permute-start | bytes 2359304 | tf_op jit(solution)/shard_map/ppermute | solution.py:22
  14.3 17.6 %collective-permute-start.2 = (bf16[384,1024]{1,0:T(8,128)(2,1)S(1)}, bf16[384,1024]{1,0:T(8,128)(2,1)}, u32[]{:S(2)}, u32[]{:S(2)}) collective-permute-start(bf16[384,1024]{1,0:T(8,128)(2,1)S(1)} %get-tuple-element.44.refs_3_.refs_6_.refs_7_), channel_id=1, source_target_pairs={{0,4},{4,8},{8,12},{12,0},{16,28},{20,16},{24,20},{28,24},{1,5},{5... | collective-permute-start | bytes 2359304 | tf_op jit(solution)/shard_map/ppermute | solution.py:22
  14.3 21.8 %collective-permute-start.1 = (bf16[384,1024]{1,0:T(8,128)(2,1)S(1)}, bf16[384,1024]{1,0:T(8,128)(2,1)S(1)}, u32[]{:S(2)}, u32[]{:S(2)}) collective-permute-start(bf16[384,1024]{1,0:T(8,128)(2,1)S(1)} %get-tuple-element.44.refs_3_.refs_6_.refs_7_), channel_id=1, source_target_pairs={{0,3},{1,0},{2,1},{3,2},{16,17},{17,18},{18,19},{19,16},{4,7},{5,4... | collective-permute-start | bytes 2359304 | tf_op jit(solution)/shard_map/ppermute | solution.py:22
  17.1 17.6 %collective-permute-start = (bf16[384,1024]{1,0:T(8,128)(2,1)S(1)}, bf16[384,1024]{1,0:T(8,128)(2,1)}, u32[]{:S(2)}, u32[]{:S(2)}) collective-permute-start(bf16[384,1024]{1,0:T(8,128)(2,1)S(1)} %get-tuple-element.44.refs_3_.refs_6_.refs_7_), channel_id=1, source_target_pairs={{0,1},{1,2},{2,3},{3,0},{16,19},{17,16},{18,17},{19,18},{4,5},{5,6... | collective-permute-start | bytes 2359304 | tf_op jit(solution)/shard_map/ppermute | solution.py:22
  19.1 49.4 %all-to-all-start = ((bf16[4,384,896]{2,1,0:T(8,128)(2,1)}), bf16[4,384,896]{2,1,0:T(8,128)(2,1)}, u32[]{:S(2)}, u32[]{:S(2)}) async-start(bf16[4,384,896]{2,1,0:T(8,128)(2,1)} %pad_maximum_fusion), calls=%async_computation | async-start | bytes 5505024 | tf_op jit(solution)/shard_map/all_to_all | solution.py:396
  32.0 15.5 %collective-permute-start.5 = (bf16[384,1024]{1,0:T(8,128)(2,1)}, bf16[384,1024]{1,0:T(8,128)(2,1)}, u32[]{:S(2)}, u32[]{:S(2)}) collective-permute-start(bf16[384,1024]{1,0:T(8,128)(2,1)} %collective-permute-done.2.refs_7_.refs_8_), channel_id=1, source_target_pairs={{0,4},{4,8},{8,12},{12,0},{16,28},{20,16},{24,20},{28,24},{1,5},{5... | collective-permute-start | bytes 2359304 | tf_op jit(solution)/shard_map/ppermute | solution.py:22
  34.7 13.5 %collective-permute-start.4 = (bf16[384,1024]{1,0:T(8,128)(2,1)}, bf16[384,1024]{1,0:T(8,128)(2,1)}, u32[]{:S(2)}, u32[]{:S(2)}) collective-permute-start(bf16[384,1024]{1,0:T(8,128)(2,1)} %collective-permute-done.refs_4_), channel_id=1, source_target_pairs={{0,1},{1,2},{2,3},{3,0},{16,19},{17,16},{18,17},{19,18},{4,5},{5,6... | collective-permute-start | bytes 2359304 | tf_op jit(solution)/shard_map/ppermute | solution.py:22
  56.2 10.0 %collective-permute-start.11 = (f32[4,384]{1,0:T(4,128)S(1)}, f32[4,384]{1,0:T(4,128)S(1)}, u32[]{:S(2)}, u32[]{:S(2)}) collective-permute-start(f32[4,384]{1,0:T(4,128)S(1)} %add_reduce_fusion.1), channel_id=1, source_target_pairs={{0,4},{4,8},{8,12},{12,0},{16,28},{20,16},{24,20},{28,24},{1,5},{5... | collective-permute-start | bytes 18440 | tf_op jit(solution)/shard_map/ppermute | solution.py:22
  56.3 9.9 %collective-permute-start.10 = (f32[4,384]{1,0:T(4,128)S(1)}, f32[4,384]{1,0:T(4,128)S(1)}, u32[]{:S(2)}, u32[]{:S(2)}) collective-permute-start(f32[4,384]{1,0:T(4,128)S(1)} %add_reduce_fusion.1), channel_id=1, source_target_pairs={{0,8},{4,12},{8,0},{12,4},{16,24},{20,28},{24,16},{28,20},{1,9},{5... | collective-permute-start | bytes 18440 | tf_op jit(solution)/shard_map/ppermute | solution.py:22
  60.8 7.0 %collective-permute-start.7 = (f32[4,512]{1,0:T(4,128)S(1)}, f32[4,512]{1,0:T(4,128)S(1)}, u32[]{:S(2)}, u32[]{:S(2)}) collective-permute-start(f32[4,512]{1,0:T(4,128)S(1)} %pad_maximum_fusion.2), channel_id=1, source_target_pairs={{0,2},{1,3},{2,0},{3,1},{16,18},{17,19},{18,16},{19,17},{4,6},{5,7... | collective-permute-start | bytes 24584 | tf_op jit(solution)/shard_map/ppermute | solution.py:22
  62.9 4.9 %collective-permute-start.8 = (f32[4,512]{1,0:T(4,128)S(1)}, f32[4,512]{1,0:T(4,128)S(1)}, u32[]{:S(2)}, u32[]{:S(2)}) collective-permute-start(f32[4,512]{1,0:T(4,128)S(1)} %pad_maximum_fusion.2), channel_id=1, source_target_pairs={{0,1},{1,2},{2,3},{3,0},{16,19},{17,16},{18,17},{19,18},{4,5},{5,6... | collective-permute-start | bytes 24584 | tf_op jit(solution)/shard_map/ppermute | solution.py:22
  68.7 29.7 %collective-permute-start.16 = (bf16[4,384,896]{2,1,0:T(8,128)(2,1)}, bf16[4,384,896]{2,1,0:T(8,128)(2,1)}, u32[]{:S(2)}, u32[]{:S(2)}) collective-permute-start(bf16[4,384,896]{2,1,0:T(8,128)(2,1)} %all-to-all-done.hidden_own), channel_id=1, source_target_pairs={{0,16},{16,0},{1,17},{17,1},{2,18},{18,2},{3,19},{19,3},{4,20},{20... | collective-permute-start | bytes 8257544 | tf_op jit(solution)/shard_map/ppermute | solution.py:26
  72.4 13.3 %collective-permute-start.17 = (bf16[384,512]{1,0:T(8,128)(2,1)S(1)}, bf16[384,512]{1,0:T(8,128)(2,1)S(1)}, u32[]{:S(2)}, u32[]{:S(2)}) collective-permute-start(bf16[384,512]{1,0:T(8,128)(2,1)S(1)} %get-tuple-element.68), channel_id=1, source_target_pairs={{0,2},{1,3},{2,0},{3,1},{16,18},{17,19},{18,16},{19,17},{4,6},{5,7... | collective-permute-start | bytes 1179656 | tf_op jit(solution)/shard_map/ppermute | solution.py:22
  74.2 13.2 %collective-permute-start.18 = (bf16[384,512]{1,0:T(8,128)(2,1)S(1)}, bf16[384,512]{1,0:T(8,128)(2,1)S(1)}, u32[]{:S(2)}, u32[]{:S(2)}) collective-permute-start(bf16[384,512]{1,0:T(8,128)(2,1)S(1)} %get-tuple-element.69), channel_id=1, source_target_pairs={{0,8},{4,12},{8,0},{12,4},{16,24},{20,28},{24,16},{28,20},{1,9},{5... | collective-permute-start | bytes 1179656 | tf_op jit(solution)/shard_map/ppermute | solution.py:22
  83.2 11.9 %collective-permute-start.12 = (bf16[384,512]{1,0:T(8,128)(2,1)}, bf16[384,512]{1,0:T(8,128)(2,1)S(1)}, u32[]{:S(2)}, u32[]{:S(2)}) collective-permute-start(bf16[384,512]{1,0:T(8,128)(2,1)} %get-tuple-element.61), channel_id=1, source_target_pairs={{0,3},{1,0},{2,1},{3,2},{16,17},{17,18},{18,19},{19,16},{4,7},{5,4... | collective-permute-start | bytes 1179656 | tf_op jit(solution)/shard_map/ppermute | solution.py:22
  84.9 10.7 %collective-permute-start.13 = (bf16[384,512]{1,0:T(8,128)(2,1)}, bf16[384,512]{1,0:T(8,128)(2,1)S(1)}, u32[]{:S(2)}, u32[]{:S(2)}) collective-permute-start(bf16[384,512]{1,0:T(8,128)(2,1)} %get-tuple-element.62), channel_id=1, source_target_pairs={{0,1},{1,2},{2,3},{3,0},{16,19},{17,16},{18,17},{19,18},{4,5},{5,6... | collective-permute-start | bytes 1179656 | tf_op jit(solution)/shard_map/ppermute | solution.py:22
  85.7 11.9 %collective-permute-start.14 = (bf16[384,512]{1,0:T(8,128)(2,1)}, bf16[384,512]{1,0:T(8,128)(2,1)}, u32[]{:S(2)}, u32[]{:S(2)}) collective-permute-start(bf16[384,512]{1,0:T(8,128)(2,1)} %get-tuple-element.63), channel_id=1, source_target_pairs={{0,12},{4,0},{8,4},{12,8},{16,20},{20,24},{24,28},{28,16},{1,13},{... | collective-permute-start | bytes 1179656 | tf_op jit(solution)/shard_map/ppermute | solution.py:22
  87.4 11.0 %collective-permute-start.15 = (bf16[384,512]{1,0:T(8,128)(2,1)}, bf16[384,512]{1,0:T(8,128)(2,1)}, u32[]{:S(2)}, u32[]{:S(2)}) collective-permute-start(bf16[384,512]{1,0:T(8,128)(2,1)} %get-tuple-element.64), channel_id=1, source_target_pairs={{0,4},{4,8},{8,12},{12,0},{16,28},{20,16},{24,20},{28,24},{1,5},{5... | collective-permute-start | bytes 1179656 | tf_op jit(solution)/shard_map/ppermute | solution.py:22
  101.9 15.2 %collective-permute-start.19 = (bf16[400,512]{1,0:T(8,128)(2,1)S(1)}, bf16[400,512]{1,0:T(8,128)(2,1)S(1)}, u32[]{:S(2)}, u32[]{:S(2)}) collective-permute-start(bf16[400,512]{1,0:T(8,128)(2,1)S(1)} %get-tuple-element.78.refs_0_.kept), channel_id=1, source_target_pairs={{0,32},{32,64},{64,96},{96,0},{16,112},{48,16},{80,48},{112,80},{1... | collective-permute-start | bytes 1228808 | tf_op jit(solution)/shard_map/ppermute | solution.py:21
  103.5 19.9 %collective-permute-start.20 = (bf16[400,512]{1,0:T(8,128)(2,1)S(1)}, bf16[400,512]{1,0:T(8,128)(2,1)S(1)}, u32[]{:S(2)}, u32[]{:S(2)}) collective-permute-start(bf16[400,512]{1,0:T(8,128)(2,1)S(1)} %get-tuple-element.78.refs_0_.kept), channel_id=1, source_target_pairs={{0,96},{32,0},{64,32},{96,64},{16,48},{48,80},{80,112},{112,16},{1... | collective-permute-start | bytes 1228808 | tf_op jit(solution)/shard_map/ppermute | solution.py:21
  105.2 16.5 %collective-permute-start.22 = (bf16[384,512]{1,0:T(8,128)(2,1)S(1)}, bf16[384,512]{1,0:T(8,128)(2,1)S(1)}, u32[]{:S(2)}, u32[]{:S(2)}) collective-permute-start(bf16[384,512]{1,0:T(8,128)(2,1)S(1)} %collective-permute-done.21.refs_3_), channel_id=1, source_target_pairs={{0,32},{32,64},{64,96},{96,0},{16,112},{48,16},{80,48},{112,80},{1... | collective-permute-start | bytes 1179656 | tf_op jit(solution)/shard_map/ppermute | solution.py:21
  105.5 18.8 %collective-permute-start.23 = (bf16[384,512]{1,0:T(8,128)(2,1)S(1)}, bf16[384,512]{1,0:T(8,128)(2,1)S(1)}, u32[]{:S(2)}, u32[]{:S(2)}) collective-permute-start(bf16[384,512]{1,0:T(8,128)(2,1)S(1)} %collective-permute-done.21.refs_3_), channel_id=1, source_target_pairs={{0,96},{32,0},{64,32},{96,64},{16,48},{48,80},{80,112},{112,16},{1... | collective-permute-start | bytes 1179656 | tf_op jit(solution)/shard_map/ppermute | solution.py:21
  117.1 12.8 %collective-permute-start.24 = (bf16[400,512]{1,0:T(8,128)(2,1)S(1)}, bf16[400,512]{1,0:T(8,128)(2,1)S(1)}, u32[]{:S(2)}, u32[]{:S(2)}) collective-permute-start(bf16[400,512]{1,0:T(8,128)(2,1)S(1)} %collective-permute-done.19.refs_1_.back), channel_id=1, source_target_pairs={{0,32},{32,64},{64,96},{96,0},{16,112},{48,16},{80,48},{112,80},{1... | collective-permute-start | bytes 1228808 | tf_op jit(solution)/shard_map/ppermute | solution.py:21
  121.7 10.9 %collective-permute-start.25 = (bf16[384,512]{1,0:T(8,128)(2,1)S(1)}, bf16[384,512]{1,0:T(8,128)(2,1)S(1)}, u32[]{:S(2)}, u32[]{:S(2)}) collective-permute-start(bf16[384,512]{1,0:T(8,128)(2,1)S(1)} %collective-permute-done.22.refs_4_), channel_id=1, source_target_pairs={{0,32},{32,64},{64,96},{96,0},{16,112},{48,16},{80,48},{112,80},{1... | collective-permute-start | bytes 1179656 | tf_op jit(solution)/shard_map/ppermute | solution.py:21
  (18 other events, 95.7 us)
